TPU v7x, 32 devices: a whole 2x2x4 slice. The times are simulated.
32 devices in a mesh: groups: 2 (over y), seq: 16 (over z, x, core).
Axes of the slice: x: 2, y: 2, z: 4, core: 2. Of those that a mesh axis runs over, the one named last changes fastest.
Arguments:
- inputs: bfloat16 [4, 8192, 1536], P('groups', 'seq'), parts along dimension 0, may hold values from -6 to 6
- conv_weight: bfloat16 [3, 1536, 768], P(None, 'seq'), may hold values from -0.09375 to 0.09375
- proj_weight: bfloat16 [1536, 768], P('seq'), may hold values from -0.21875 to 0.21875
- cotangent: bfloat16 [4, 8192, 1536], P('groups', 'seq'), parts along dimension 0, may hold values from -6 to 6
Outputs:
- outputs: bfloat16 [4, 8192, 1536], P('groups', 'seq'), parts along dimension 0
- input_grad: bfloat16 [4, 8192, 1536], P('groups', 'seq'), parts along dimension 0
- conv_grad: float32 [3072, 3, 768], P(('groups', 'seq')), parts along dimension 0
- proj_grad: float32 [3072, 768], P(('groups', 'seq')), parts along dimension 0
There are 2 independent parts, one for each index of `groups`. A program takes and returns all parts, laid end to end along the dimension named above; an argument that names none is the same for every part. Nothing has to cross between parts.
All inputs are finite; a program needn't handle non-finite values.
Results may differ from a plain program's by a relative error of at most 0.0051.
Values may be sent and summed in bfloat16 or wider, within the bound.
A program may use at most 128 MiB of HBM per device.

v0:
```python
import jax
import jax.numpy as jnp
from jax import lax
from jax.sharding import PartitionSpec as P

L = 8192


def from_behind(block, axis, distance):
    devices = range(lax.axis_size(axis))
    route = [(i - distance, i) for i in devices if i - distance in devices]
    return lax.ppermute(block, axis, route)


def gelu_grad(point, upstream):
    return jax.vjp(jax.nn.gelu, point)[1](upstream)[0]


def shards(inputs, conv_weight, proj_weight, cotangent):
    batch, local_len, chans = inputs.shape
    devices = lax.axis_size("seq")
    stride = devices // 8
    scale = 1.0 / float(batch * L) ** 0.5
    acted = jax.nn.gelu(inputs.astype(jnp.float32)).astype(jnp.bfloat16)
    conv_weight, proj_weight = (
        lax.all_gather(conv_weight, "seq", axis=1, tiled=True),
        lax.all_gather(proj_weight, "seq", axis=0, tiled=True),
    )
    hid = conv_weight.shape[2]
    acted_rows = acted.reshape(-1, chans)
    before = from_behind(acted, "seq", stride)
    after = from_behind(acted, "seq", -stride)
    hidden = jnp.dot(before.reshape(-1, chans), conv_weight[0], preferred_element_type=jnp.float32)
    hidden = hidden + jnp.dot(acted_rows, conv_weight[1], preferred_element_type=jnp.float32)
    hidden = hidden + jnp.dot(
        after.reshape(-1, chans), conv_weight[2], preferred_element_type=jnp.float32
    )
    gated = jax.nn.gelu(hidden).astype(jnp.bfloat16)
    outputs = (
        inputs.reshape(-1, chans).astype(jnp.float32)
        + jnp.dot(gated, proj_weight.T, preferred_element_type=jnp.float32)
    ).astype(jnp.bfloat16)
    cot_rows = cotangent.reshape(-1, chans)
    gated_grad = jnp.dot(cot_rows, proj_weight, preferred_element_type=jnp.float32)
    hidden_grad = gelu_grad(hidden, gated_grad).astype(jnp.bfloat16)
    grad_blocks = hidden_grad.reshape(batch, local_len, hid)
    grad_later = from_behind(grad_blocks, "seq", -stride).reshape(-1, hid)
    grad_earlier = from_behind(grad_blocks, "seq", stride).reshape(-1, hid)
    acted_grad = jnp.dot(grad_later, conv_weight[0].T, preferred_element_type=jnp.float32)
    acted_grad = acted_grad + jnp.dot(
        hidden_grad, conv_weight[1].T, preferred_element_type=jnp.float32
    )
    acted_grad = acted_grad + jnp.dot(
        grad_earlier, conv_weight[2].T, preferred_element_type=jnp.float32
    )
    input_grad = (
        cot_rows.astype(jnp.float32)
        + gelu_grad(inputs.reshape(-1, chans).astype(jnp.float32), acted_grad)
    ).astype(jnp.bfloat16)
    tap_grads = (grad_later, hidden_grad, grad_earlier)
    share = chans // devices
    local_terms = [
        jnp.dot(acted_rows.T, piece, preferred_element_type=jnp.float32) for piece in tap_grads
    ]
    local_terms.append(jnp.dot(cot_rows.T, gated, preferred_element_type=jnp.float32))
    stacked = jnp.stack(local_terms, axis=1)
    received = lax.all_to_all(stacked, "seq", split_axis=0, concat_axis=0, tiled=True)
    summed = jnp.sum(received.reshape(devices, share, 4, received.shape[2]), axis=0)
    conv_sum = summed[:, 0:3, :]
    proj_sum = summed[:, 3, :]
    return (
        outputs.reshape(batch, local_len, chans),
        input_grad.reshape(batch, local_len, chans),
        conv_sum * scale,
        proj_sum * scale,
    )


def solution(mesh):
    return jax.shard_map(
        shards,
        mesh=mesh,
        in_specs=(
            P("groups", "seq", None),
            P(None, "seq", None),
            P("seq", None),
            P("groups", "seq", None),
        ),
        out_specs=(
            P("groups", "seq", None),
            P("groups", "seq", None),
            P(("groups", "seq"), None, None),
            P(("groups", "seq"), None),
        ),
        check_vma=False,
    )
```

profile of v0, /device:TPU:15, one launch (start us, length us, event | category | flops | bytes accessed | tf_op | source)
XLA Modules:
  0.0 772.2 jit_solution(15523567253440921126)
XLA Ops:
  7.2 0.0 all-gather.5.cloned.1.call-start
  7.2 0.7 all-gather.5.cloned.1.call-update
  7.9 0.0 all-gather.3.cloned.1.call-start
  7.9 0.7 all-gather.3.cloned.1.call-update
  8.6 3.6 fusion.15
  12.2 3.2 collective-permute-start
  15.4 2.1 collective-permute-start.1
  17.5 106.9 %all-gather.5.cloned.1.call-done = bf16[1536,768]{1,0:T(8,128)(2,1)} async-done(((bf16[96,768]{1,0:T(8,128)(2,1)}), bf16[1536,768]{1,0:T(8,128)(2,1)}) %all-gather.5.cloned.1.call-update) | async-done | bytes 2359312 | tf_op jit(solution)/shard_map/all_gather | solution.py:27
  124.4 6.9 fusion.34
  131.3 32.3 %collective-permute-done = bf16[2,512,1536]{2,1,0:T(8,128)(2,1)} collective-permute-done((bf16[2,512,1536]{2,1,0:T(8,128)(2,1)S(1)}, bf16[2,512,1536]{2,1,0:T(8,128)(2,1)}, u32[]{:S(2)}, u32[]{:S(2)}) %collective-permute-start) | collective-permute-done | bytes 3145760 | tf_op jit(solution)/shard_map/ppermute | solution.py:12
  163.6 33.0 %all-gather.3.cloned.1.call-done = bf16[3,1536,768]{2,1,0:T(8,128)(2,1)} async-done(((bf16[3,96,768]{2,1,0:T(8,128)(2,1)}), bf16[3,1536,768]{2,1,0:T(8,128)(2,1)}) %all-gather.3.cloned.1.call-update) | async-done | bytes 7077904 | tf_op jit(solution)/shard_map/all_gather | solution.py:26
  196.6 0.0 copy-start.1
  196.6 5.4 fusion.27
  202.0 0.0 copy-done.1
  202.0 0.0 copy-start.12
  202.0 2.6 fusion.29
  204.6 0.0 collective-permute-done.1
  204.6 0.0 copy-done.12
  204.6 6.2 fusion.25
  210.8 0.0 copy-start.5
  210.8 0.0 copy-start.10
  210.9 0.0 copy-start.2
  210.9 5.5 collective-permute-start.3
  216.3 2.2 collective-permute-start.2
  218.5 2.8 convolution_bitcast_fusion.2
  221.3 0.0 copy-done.5
  221.3 0.0 copy-done.10
  221.3 0.0 copy-done.2
  221.3 0.0 copy-start
  221.4 3.2 convolution_bitcast_fusion
  224.6 59.4 %collective-permute-done.3 = bf16[2,512,768]{2,1,0:T(8,128)(2,1)S(1)} collective-permute-done((bf16[2,512,768]{2,1,0:T(8,128)(2,1)S(1)}, bf16[2,512,768]{2,1,0:T(8,128)(2,1)S(1)}, u32[]{:S(2)}, u32[]{:S(2)}) %collective-permute-start.3) | collective-permute-done | bytes 1572896 | tf_op jit(solution)/shard_map/ppermute | solution.py:12
  284.0 0.0 copy-done
  284.0 4.0 convolution_bitcast_fusion.1
  288.1 0.0 copy-done.6
  288.1 0.0 collective-permute-done.2
  288.1 0.0 copy-start.8
  288.1 1.2 copy-done.8
  289.3 14.4 %convolution_bitcast_fusion.3 = f32[1536,1,768]{2,0,1:T(8,128)S(1)} fusion(bf16[2,512,768]{2,1,0:T(8,128)(2,1)S(1)} %collective-permute-done.2, bf16[2,512,1536]{2,1,0:T(8,128)(2,1)S(1)} %copy-done), kind=kOutput, calls=%fused_computation.30 | convolution fusion | flops 2431647744 | bytes 9437184 | tf_op jit(solution)/shard_map/dot_general | solution.py:63
  303.6 1.9 pad_maximum_fusion
  305.6 34.4 %copy.18 = f32[1536,4,768]{2,1,0:T(4,128)} copy(f32[1536,4,768]{2,0,1:T(8,128)S(1)} %pad_maximum_fusion) | data formatting | bytes 37748736 | tf_op jit(solution)/shard_map/stack | solution.py:66
  339.9 5.3 all-to-all-start
  345.3 0.0 copy-start.11
  345.3 0.0 slice-start
  345.3 4.9 fusion.28
  350.2 0.0 copy-done.4
  350.2 0.0 copy-done.11
  350.2 0.0 slice-start.1
  350.3 0.0 copy-start.9
  350.3 4.3 fusion.16
  354.5 0.0 slice-done
  354.5 0.0 slice-done.1
  354.5 0.0 copy-done.9
  354.5 0.0 copy-start.3
  354.6 0.0 copy-start.7
  354.6 4.7 fusion.26
  359.2 0.0 copy-done.3
  359.2 0.0 copy-done.7
  359.2 9.7 %fusion.7 = bf16[1024,1536]{1,0:T(8,128)(2,1)} fusion(bf16[2,512,1536]{2,1,0:T(8,128)(2,1)S(1)} %copy-done, f32[1024,1536]{1,0:T(8,128)} %fusion.26, f32[1024,1536]{1,0:T(8,128)S(1)} %fusion.28, bf16[1024,1536]{1,0:T(8,128)(2,1)S(1)} %bitcast.79, bf16[1024,768]{1,0:T(8,128)(2,1)S(1)} %bitcast.82, bf16[3,1536,768]{2,1,0:T(8,128)(2,1)S(1)} %bitcast.76), kind=kOutput, calls=%fused_computation.11 | convolution fusion | flops 2455240704 | bytes 25952256 | tf_op jit(solution)/shard_map/dot_general | solution.py:53
  368.9 383.4 %all-to-all-done = f32[1536,4,768]{2,1,0:T(4,128)} async-done(((f32[1536,4,768]{2,1,0:T(4,128)}), f32[1536,4,768]{2,1,0:T(4,128)}, u32[]{:S(2)}, u32[]{:S(2)}) %all-to-all-start) | async-done | bytes 18874400 | tf_op jit(solution)/shard_map/all_to_all | solution.py:67
  752.3 10.4 %reduce_sum.9 = f32[96,4,768]{2,1,0:T(4,128)S(1)} reduce(f32[16,96,4,768]{3,2,1,0:T(4,128)} %bitcast.20, f32[]{:T(128)} %constant.14.clone.1), dimensions={0}, to_apply=%region_0.0 | reduce | flops 4423680 | bytes 20054020 | tf_op jit(solution)/shard_map/reduce_sum | solution.py:68
  762.8 0.3 slice_multiply_fusion
  763.0 0.4 slice_multiply_fusion.1
  763.4 1.1 copy.19
  764.5 0.7 copy.25
  (3 shorter events, 0.0 us)
Async XLA Ops:
  7.2 117.2 %all-gather.5.cloned.1.call-start = ((), (), s32[]{:S(2)}) async-start(), calls=%async_computation.2 | async-start | bytes 2506752 | tf_op jit(solution)/shard_map/all_gather | solution.py:27
  7.9 188.7 %all-gather.3.cloned.1.call-start = ((), (), s32[]{:S(2)}) async-start(), calls=%async_computation.1 | async-start | bytes 7520256 | tf_op jit(solution)/shard_map/all_gather | solution.py:26
  12.2 151.4 %collective-permute-start = (bf16[2,512,1536]{2,1,0:T(8,128)(2,1)S(1)}, bf16[2,512,1536]{2,1,0:T(8,128)(2,1)}, u32[]{:S(2)}, u32[]{:S(2)}) collective-permute-start(bf16[2,512,1536]{2,1,0:T(8,128)(2,1)S(1)} %fusion.15), channel_id=1, source_target_pairs={{0,2},{1,3},{2,4},{3,5},{4,6},{5,7},{6,8},{7,9},{8,10},{9,11},{10,... | collective-permute-start | bytes 9437192 | tf_op jit(solution)/shard_map/ppermute | solution.py:12
  15.4 189.2 %collective-permute-start.1 = (bf16[2,512,1536]{2,1,0:T(8,128)(2,1)S(1)}, bf16[2,512,1536]{2,1,0:T(8,128)(2,1)}, u32[]{:S(2)}, u32[]{:S(2)}) collective-permute-start(bf16[2,512,1536]{2,1,0:T(8,128)(2,1)S(1)} %fusion.15), channel_id=1, source_target_pairs={{2,0},{3,1},{4,2},{5,3},{6,4},{7,5},{8,6},{9,7},{10,8},{11,9},{12,... | collective-permute-start | bytes 9437192 | tf_op jit(solution)/shard_map/ppermute | solution.py:12
  196.6 5.4 copy-start.1
  202.0 2.6 copy-start.12
  210.8 10.5 %copy-start.5 = (bf16[1024,768]{1,0:T(8,128)(2,1)}, bf16[1024,768]{1,0:T(8,128)(2,1)S(1)}, u32[]{:S(2)}) copy-start(bf16[1024,768]{1,0:T(8,128)(2,1)S(1)} %get-tuple-element.8) | copy-start | bytes 4718596
  210.8 10.5 %copy-start.10 = (f32[1024,768]{1,0:T(8,128)}, f32[1024,768]{1,0:T(8,128)S(1)}, u32[]{:S(2)}) copy-start(f32[1024,768]{1,0:T(8,128)S(1)} %get-tuple-element.9) | copy-start | bytes 9437188
  210.9 10.5 %copy-start.2 = (bf16[2,512,1536]{2,1,0:T(8,128)(2,1)S(1)}, bf16[2,512,1536]{2,1,0:T(8,128)(2,1)}, u32[]{:S(2)}) copy-start(bf16[2,512,1536]{2,1,0:T(8,128)(2,1)} %param.7) | copy-start | bytes 9437188
  210.9 73.2 %collective-permute-start.3 = (bf16[2,512,768]{2,1,0:T(8,128)(2,1)S(1)}, bf16[2,512,768]{2,1,0:T(8,128)(2,1)S(1)}, u32[]{:S(2)}, u32[]{:S(2)}) collective-permute-start(bf16[2,512,768]{2,1,0:T(8,128)(2,1)S(1)} %bitcast.80), channel_id=1, source_target_pairs={{0,2},{1,3},{2,4},{3,5},{4,6},{5,7},{6,8},{7,9},{8,10},{9,11},{10,... | collective-permute-start | bytes 4718600 | tf_op jit(solution)/shard_map/ppermute | solution.py:12
  216.3 71.7 %collective-permute-start.2 = (bf16[2,512,768]{2,1,0:T(8,128)(2,1)S(1)}, bf16[2,512,768]{2,1,0:T(8,128)(2,1)S(1)}, u32[]{:S(2)}, u32[]{:S(2)}) collective-permute-start(bf16[2,512,768]{2,1,0:T(8,128)(2,1)S(1)} %bitcast.81), channel_id=1, source_target_pairs={{2,0},{3,1},{4,2},{5,3},{6,4},{7,5},{8,6},{9,7},{10,8},{11,9},{12,... | collective-permute-start | bytes 4718600 | tf_op jit(solution)/shard_map/ppermute | solution.py:12
  221.3 62.7 %copy-start = (bf16[2,512,1536]{2,1,0:T(8,128)(2,1)S(1)}, bf16[2,512,1536]{2,1,0:T(8,128)(2,1)}, u32[]{:S(2)}) copy-start(bf16[2,512,1536]{2,1,0:T(8,128)(2,1)} %param.4) | copy-start | bytes 9437188
  284.0 4.0 copy-start.6
  288.1 1.2 copy-start.8
  339.9 412.4 %all-to-all-start = ((f32[1536,4,768]{2,1,0:T(4,128)}), f32[1536,4,768]{2,1,0:T(4,128)}, u32[]{:S(2)}, u32[]{:S(2)}) async-start(f32[1536,4,768]{2,1,0:T(4,128)} %copy.18), calls=%async_computation | async-start | bytes 37748736 | tf_op jit(solution)/shard_map/all_to_all | solution.py:67
  345.3 5.0 copy-start.4
  345.3 5.0 copy-start.11
  345.3 9.2 %slice-start = ((s8[7077888]{0:T(1024)(128)(4,1)}), s8[4194304]{0:T(1024)(128)(4,1)S(1)}, s32[]{:S(2)}) async-start(s8[7077888]{0:T(1024)(128)(4,1)} %bitcast.75), calls=%async_computation.3 | async-start | bytes 8388608
  350.2 4.3 slice-start.1
  350.3 4.3 copy-start.9
  354.5 4.7 copy-start.3
  354.6 4.7 copy-start.7
Sparse Core Ops, SparseCore 0:
  10.3 114.0 all-gather.4
  126.7 69.8 all-gather.2
where the time goes:
time: 775 us; the launch traced here: 772 us
  waiting for transfers between devices  616 us (79%)
  matrix products  69 us (9%)
  local copies, waits for them, and re-layouts  37.4 us (5%)
  starting transfers between devices  18.3 us (2%)
  other arithmetic  16.6 us (2%)
  between operations  14.5 us (2%)
    all_to_all x1, waiting for transfers between devices, shards(): lax.all_to_all(stacked, 'seq', split_axis=0, concat_axis=0, tiled=True)  383 us
    all_gather x1, waiting for transfers between devices, shards(): lax.all_gather(proj_weight, 'seq', axis=0, tiled=True)  107 us
    ppermute x4, waiting for transfers between devices, from_behind(): return lax.ppermute(block, axis, route)  91.8 us
    another operation x1, local copies, waits for them, and re-layouts, shards(): stacked = jnp.stack(local_terms, axis=1)  34.4 us
    all_gather x1, waiting for transfers between devices, shards(): lax.all_gather(conv_weight, 'seq', axis=1, tiled=True)  33 us
    dot_general x3, matrix products, shards(): jnp.dot(acted_rows.T, piece, preferred_element_type=jnp.float32)  21.2 us
  transfers between devices with their start and end apart: 7, of which 5 were waited for; matrix products, arithmetic and copies ran while one was open for 7% of the time, Pallas kernels for 0%

commit v1 on v0

--- a/solution.py
+++ b/solution.py
@@ -1,6 +1,10 @@
+import functools
+
 import jax
 import jax.numpy as jnp
 from jax import lax
+from jax.experimental import pallas as pl
+from jax.experimental.pallas import tpu as pltpu
 from jax.sharding import PartitionSpec as P
 
 L = 8192
@@ -76,9 +80,470 @@
     )
 
 
+F32 = jnp.float32
+BF16 = jnp.bfloat16
+MESH = pl.DeviceIdType.MESH
+VMEM = pl.BlockSpec(memory_space=pltpu.VMEM)
+HBM = pl.BlockSpec(memory_space=pl.ANY)
+SEQ = 16
+CHUNKS = 4
+COEF = 0.7978845608028654
+CUBE = 0.044715
+
+
+def place():
+    s = lax.axis_index("seq")
+    return s // 4, (s // 2) % 2, s % 2
+
+
+def index(z, x, core):
+    return (z * 2 + x) * 2 + core
+
+
+def copy_to(src, dst, send, recv, target):
+    return pltpu.make_async_remote_copy(
+        src_ref=src, dst_ref=dst, send_sem=send, recv_sem=recv,
+        device_id={"seq": target}, device_id_type=MESH,
+    )
+
+
+def greet(targets):
+    barrier = pltpu.get_barrier_semaphore()
+    for target in targets:
+        pl.semaphore_signal(barrier, inc=1, device_id={"seq": target}, device_id_type=MESH)
+    pl.semaphore_wait(barrier, len(targets))
+
+
+def gelu_parts(v):
+    t = jnp.tanh(COEF * (v + CUBE * v * v * v))
+    half = 0.5 * (1.0 + t)
+    return half * v, half + (0.5 * COEF) * v * (1.0 - t * t) * (1.0 + (3.0 * CUBE) * v * v)
+
+
+def params(cid, mib=56):
+    return pltpu.CompilerParams(
+        collective_id=cid, has_side_effects=True, vmem_limit_bytes=mib * 1024 * 1024
+    )
+
+
+def gather_kernel(w_ref, x_ref, full_ref, acted_ref, own_sem, zs, zr, xs, xr, cs, cr):
+    z, x, core = place()
+    share = w_ref.shape[1]
+    zt = [lax.rem(z + d, 4) for d in range(4)]
+    zf = [lax.rem(z + 4 - d, 4) for d in range(4)]
+
+    def rows(zz, xx, cc):
+        start = pl.multiple_of(index(zz, xx, cc) * share, share)
+        return full_ref.at[:, pl.ds(start, share), :]
+
+    greet([index(zt[d], x, core) for d in (1, 2, 3)]
+          + [index(z, 1 - x, core), index(z, x, 1 - core)])
+    mine = rows(z, x, core)
+    copies = []
+    for d in (1, 3, 2):
+        copies.append(copy_to(w_ref, mine, zs.at[d], zr.at[d], index(zt[d], x, core)))
+        copies[-1].start()
+    zc = dict(zip((1, 3, 2), copies))
+
+    def to_x(j, src):
+        c = copy_to(src, rows(zf[j], x, core), xs.at[j], xr.at[j], index(z, 1 - x, core))
+        c.start()
+        return c
+
+    def to_core(j, src, xx):
+        c = copy_to(src, rows(zf[j % 4], xx, core), cs.at[j], cr.at[j], index(z, x, 1 - core))
+        c.start()
+        return c
+
+    xc = {0: to_x(0, w_ref)}
+    cc = {0: to_core(0, w_ref, x)}
+    own = pltpu.make_async_copy(w_ref, mine, own_sem)
+    own.start()
+
+    tile = 64
+
+    def act(i, carry):
+        r = pl.ds(pl.multiple_of(i * tile, tile), tile)
+        v = x_ref[r, :].astype(F32)
+        t = jnp.tanh(COEF * (v + CUBE * v * v * v))
+        acted_ref[r, :] = (0.5 * v * (1.0 + t)).astype(BF16)
+        return carry
+
+    lax.fori_loop(0, x_ref.shape[0] // tile, act, 0)
+
+    def take_z(j):
+        zc[j].wait_recv()
+        src = rows(zf[j], x, core)
+        xc[j] = to_x(j, src)
+        cc[j] = to_core(j, src, x)
+
+    def take_x(j):
+        xc[j].wait_recv()
+        cc[4 + j] = to_core(4 + j, rows(zf[j], 1 - x, core), 1 - x)
+
+    take_z(1)
+    take_z(3)
+    take_x(0)
+    take_z(2)
+    take_x(1)
+    take_x(3)
+    take_x(2)
+    for j in range(8):
+        cc[j].wait_recv()
+    own.wait()
+    for j in (1, 2, 3):
+        zc[j].wait_send()
+    for j in range(4):
+        xc[j].wait_send()
+    for j in range(8):
+        cc[j].wait_send()
+
+
+def gather(w4, flat):
+    taps, share, hid = w4.shape
+    dma = pltpu.SemaphoreType.DMA
+    return pl.pallas_call(
+        gather_kernel,
+        out_shape=(
+            jax.ShapeDtypeStruct((taps, share * SEQ, hid), BF16),
+            jax.ShapeDtypeStruct(flat.shape, BF16),
+        ),
+        in_specs=[HBM, VMEM],
+        out_specs=(HBM, VMEM),
+        scratch_shapes=[dma, dma((4,)), dma((4,)), dma((4,)), dma((4,)), dma((8,)), dma((8,))],
+        compiler_params=params(0),
+        name="gather_weights",
+    )(w4, flat)
+
+
+def forward_kernel(acted_ref, w_ref, cot_ref, gated_ref, hg_ref,
+                   out_a, in_a, out_s, in_s, part, gg, zs, zr, xs, xr):
+    z, x, core = place()
+    up = x == 1
+    sends = jnp.logical_or(jnp.logical_and(up, z < 3), jnp.logical_and(x == 0, z > 0))
+    takes = jnp.logical_or(jnp.logical_and(up, z > 0), jnp.logical_and(x == 0, z < 3))
+    step = 2 * x - 1
+    ahead = index(lax.rem(z + step + 4, 4), x, core)
+    behind = index(lax.rem(z - step + 4, 4), x, core)
+    across = index(z, 1 - x, core)
+    greet([ahead, behind, across])
+    n = acted_ref.shape[0] // CHUNKS
+    tap_far = 2 - 2 * x
+    tap_near = 2 * x
+
+    def rows(i):
+        return pl.ds(pl.multiple_of(i * n, n), n)
+
+    def z_copy(i):
+        return copy_to(out_a.at[i], in_a.at[i], zs.at[i], zr.at[i], ahead)
+
+    def x_copy(i):
+        return copy_to(out_s.at[i], in_s.at[i], xs.at[i], xr.at[i], across)
+
+    def far(i, carry):
+        out_a[i] = jnp.dot(acted_ref[rows(i), :], w_ref[tap_far], preferred_element_type=F32).astype(BF16)
+
+        @pl.when(sends)
+        def _():
+            z_copy(i).start()
+        return carry
+
+    lax.fori_loop(0, CHUNKS, far, 0)
+
+    def near(i, carry):
+        part[i] = jnp.dot(acted_ref[rows(i), :], w_ref[tap_near], preferred_element_type=F32)
+        gg[i] = jnp.dot(cot_ref[rows(i), :], w_ref[3], preferred_element_type=F32)
+        return carry
+
+    lax.fori_loop(0, CHUNKS, near, 0)
+
+    def combine(i, carry):
+        @pl.when(takes)
+        def _():
+            z_copy(i).wait_recv()
+            part[i] = part[i] + in_a[i].astype(F32)
+        out_s[i] = part[i].astype(BF16)
+        x_copy(i).start()
+        part[i] = jnp.dot(acted_ref[rows(i), :], w_ref[1], preferred_element_type=F32)
+        return carry
+
+    lax.fori_loop(0, CHUNKS, combine, 0)
+
+    def finish(i, carry):
+        x_copy(i).wait_recv()
+        hidden = part[i] + in_s[i].astype(F32)
+        value, slope = gelu_parts(hidden)
+        gated_ref[rows(i), :] = value.astype(BF16)
+        hg_ref[rows(i), :] = (gg[i] * slope).astype(BF16)
+        return carry
+
+    lax.fori_loop(0, CHUNKS, finish, 0)
+
+    def drain(i, carry):
+        x_copy(i).wait_send()
+
+        @pl.when(sends)
+        def _():
+            z_copy(i).wait_send()
+        return carry
+
+    lax.fori_loop(0, CHUNKS, drain, 0)
+
+
+def forward(acted, w4, cot):
+    m = acted.shape[0]
+    hid = w4.shape[2]
+    dma = pltpu.SemaphoreType.DMA
+    block = (CHUNKS, m // CHUNKS, hid)
+    return pl.pallas_call(
+        forward_kernel,
+        out_shape=(jax.ShapeDtypeStruct((m, hid), BF16),) * 2,
+        in_specs=[VMEM] * 3,
+        out_specs=(VMEM, VMEM),
+        scratch_shapes=[pltpu.VMEM(block, BF16)] * 4 + [pltpu.VMEM(block, F32)] * 2
+        + [dma((CHUNKS,))] * 4,
+        compiler_params=params(1),
+        name="forward_halo",
+    )(acted, w4, cot)
+
+
+def halo_kernel(hg_ref, later_ref, earlier_ref, from_x, from_z, zs, zr, xs, xr):
+    z, x, core = place()
+    even = x == 0
+    sends = jnp.logical_or(jnp.logical_and(even, z < 3), jnp.logical_and(x == 1, z > 0))
+    takes = jnp.logical_or(jnp.logical_and(even, z > 0), jnp.logical_and(x == 1, z < 3))
+    step = 1 - 2 * x
+    ahead = index(lax.rem(z + step + 4, 4), x, core)
+    behind = index(lax.rem(z - step + 4, 4), x, core)
+    across = index(z, 1 - x, core)
+    greet([ahead, behind, across])
+    n = hg_ref.shape[0] // CHUNKS
+
+    def rows(i):
+        return pl.ds(pl.multiple_of(i * n, n), n)
+
+    def x_copy(i):
+        return copy_to(hg_ref.at[rows(i), :], from_x.at[i], xs.at[i], xr.at[i], across)
+
+    def z_copy(i):
+        return copy_to(from_x.at[i], from_z.at[i], zs.at[i], zr.at[i], ahead)
+
+    def launch(i, carry):
+        x_copy(i).start()
+        return carry
+
+    lax.fori_loop(0, CHUNKS, launch, 0)
+
+    def onward(i, carry):
+        x_copy(i).wait_recv()
+
+        @pl.when(sends)
+        def _():
+            z_copy(i).start()
+        return carry
+
+    lax.fori_loop(0, CHUNKS, onward, 0)
+
+    def finish(i, carry):
+        @pl.when(takes)
+        def _():
+            z_copy(i).wait_recv()
+
+        @pl.when(jnp.logical_not(takes))
+        def _():
+            from_z[i] = jnp.zeros(from_z.shape[1:], BF16)
+
+        @pl.when(even)
+        def _():
+            later_ref[rows(i), :] = from_x[i]
+            earlier_ref[rows(i), :] = from_z[i]
+
+        @pl.when(x == 1)
+        def _():
+            later_ref[rows(i), :] = from_z[i]
+            earlier_ref[rows(i), :] = from_x[i]
+        return carry
+
+    lax.fori_loop(0, CHUNKS, finish, 0)
+
+    def drain(i, carry):
+        x_copy(i).wait_send()
+
+        @pl.when(sends)
+        def _():
+            z_copy(i).wait_send()
+        return carry
+
+    lax.fori_loop(0, CHUNKS, drain, 0)
+
+
+def halo(hg):
+    m, hid = hg.shape
+    dma = pltpu.SemaphoreType.DMA
+    block = (CHUNKS, m // CHUNKS, hid)
+    return pl.pallas_call(
+        halo_kernel,
+        out_shape=(jax.ShapeDtypeStruct((m, hid), BF16),) * 2,
+        in_specs=[VMEM],
+        out_specs=(VMEM, VMEM),
+        scratch_shapes=[pltpu.VMEM(block, BF16)] * 2 + [dma((CHUNKS,))] * 4,
+        compiler_params=params(2),
+        name="backward_halo",
+    )(hg)
+
+
+ORDER = (2, 1, 3, 0)
+
+
+def reduce_kernel(scale, acted_ref, cot_ref, later_ref, hg_ref, earlier_ref, gated_ref, out_ref,
+                  give, keep, got, acc, x_out, x_in, z_out, z_in, cs, cr, xs, xr, zs, zr):
+    z, x, core = place()
+    share = out_ref.shape[1]
+    zt = [lax.rem(z + d, 4) for d in range(4)]
+    across = index(z, 1 - x, core)
+    other = index(z, x, 1 - core)
+    greet([index(zt[d], x, core) for d in (1, 2, 3)] + [across, other])
+    taps = (later_ref, hg_ref, earlier_ref, gated_ref)
+    wide = 4 * share
+    tile = 256
+    hid = hg_ref.shape[1]
+
+    def core_copy(s):
+        return copy_to(give.at[s % 2], got.at[s], cs.at[s], cr.at[s], other)
+
+    def x_copy(s):
+        return copy_to(x_out.at[s], x_in.at[s], xs.at[s], xr.at[s], across)
+
+    def z_copy(s):
+        return copy_to(z_out.at[s], z_in.at[s], zs.at[s], zr.at[s], index(zt[ORDER[s]], x, core))
+
+    def compute(s):
+        cols = pl.ds(pl.multiple_of(zt[ORDER[s]] * wide, wide), wide)
+        for k in range(4):
+            left = cot_ref if k == 3 else acted_ref
+
+            def part(i, carry, k=k, left=left):
+                t = pl.ds(pl.multiple_of(i * tile, tile), tile)
+                p = lax.dot_general(left[:, cols], taps[k][:, t], (((0,), (0,)), ((), ())),
+                                    preferred_element_type=F32)
+                for xx in range(2):
+                    lo = p[2 * xx * share:(2 * xx + 1) * share]
+                    hi = p[(2 * xx + 1) * share:(2 * xx + 2) * share]
+                    keep[s % 2, xx, k, :, t] = jnp.where(core == 0, lo, hi)
+                    give[s % 2, xx, k, :, t] = jnp.where(core == 0, hi, lo)
+                return carry
+
+            lax.fori_loop(0, hid // tile, part, 0)
+        core_copy(s).start()
+
+    def to_across(s):
+        core_copy(s).wait_recv()
+
+        def add(k, carry):
+            x_out[s, k] = (keep[s % 2, 1 - x, k] + got[s, 1 - x, k]).astype(BF16)
+            acc[s, k] = keep[s % 2, x, k] + got[s, x, k]
+            return carry
+
+        lax.fori_loop(0, 4, add, 0)
+        x_copy(s).start()
+
+    def to_z(s):
+        x_copy(s).wait_recv()
+
+        def add(k, carry):
+            z_out[s, k] = (acc[s, k] + x_in[s, k].astype(F32)).astype(BF16)
+            return carry
+
+        lax.fori_loop(0, 4, add, 0)
+        z_copy(s).start()
+
+    compute(0)
+    compute(1)
+    to_across(0)
+    core_copy(0).wait_send()
+    compute(2)
+    to_across(1)
+    core_copy(1).wait_send()
+    compute(3)
+    to_across(2)
+    to_z(0)
+    to_across(3)
+    to_z(1)
+    to_z(2)
+    x_copy(3).wait_recv()
+    for s in range(3):
+        z_copy(s).wait_recv()
+
+    def total(k, carry):
+        own = acc[3, k] + x_in[3, k].astype(F32)
+        for s in range(3):
+            own = own + z_in[s, k].astype(F32)
+        out_ref[k] = own * scale
+        return carry
+
+    lax.fori_loop(0, 4, total, 0)
+    core_copy(2).wait_send()
+    core_copy(3).wait_send()
+    for s in range(4):
+        x_copy(s).wait_send()
+    for s in range(3):
+        z_copy(s).wait_send()
+
+
+def reduce_grads(scale, acted, cot, later, hg, earlier, gated):
+    chans, hid = acted.shape[1], hg.shape[1]
+    share = chans // SEQ
+    dma = pltpu.SemaphoreType.DMA
+    pair = (2, 4, share, hid)
+    return pl.pallas_call(
+        functools.partial(reduce_kernel, scale),
+        out_shape=jax.ShapeDtypeStruct((4, share, hid), F32),
+        in_specs=[VMEM] * 6,
+        out_specs=VMEM,
+        scratch_shapes=[
+            pltpu.VMEM((2,) + pair, F32),
+            pltpu.VMEM((2,) + pair, F32),
+            pltpu.VMEM((4,) + pair, F32),
+            pltpu.VMEM((4, 4, share, hid), F32),
+            pltpu.VMEM((4, 4, share, hid), BF16),
+            pltpu.VMEM((4, 4, share, hid), BF16),
+            pltpu.VMEM((3, 4, share, hid), BF16),
+            pltpu.VMEM((3, 4, share, hid), BF16),
+            dma((4,)), dma((4,)), dma((4,)), dma((4,)), dma((3,)), dma((3,)),
+        ],
+        compiler_params=params(3),
+        name="reduce_grads",
+    )(acted, cot, later, hg, earlier, gated)
+
+
+def pair_shards(inputs, conv_weight, proj_weight, cotangent):
+    batch, local_len, chans = inputs.shape
+    scale = 1.0 / float(batch * L) ** 0.5
+    rows = inputs.reshape(-1, chans)
+    cot = cotangent.reshape(-1, chans)
+    full, acted = gather(jnp.concatenate([conv_weight, proj_weight[None]], axis=0), rows)
+    gated, hg = forward(acted, full, cot)
+    later, earlier = halo(hg)
+    outputs = (
+        rows.astype(F32) + jnp.dot(gated, full[3].T, preferred_element_type=F32)
+    ).astype(BF16)
+    acted_grad = jnp.dot(later, full[0].T, preferred_element_type=F32)
+    acted_grad = acted_grad + jnp.dot(hg, full[1].T, preferred_element_type=F32)
+    acted_grad = acted_grad + jnp.dot(earlier, full[2].T, preferred_element_type=F32)
+    input_grad = (cot.astype(F32) + gelu_grad(rows.astype(F32), acted_grad)).astype(BF16)
+    grads = reduce_grads(scale, acted, cot, later, hg, earlier, gated)
+    return (
+        outputs.reshape(batch, local_len, chans),
+        input_grad.reshape(batch, local_len, chans),
+        grads[:3].transpose(1, 0, 2),
+        grads[3],
+    )
+
+
 def solution(mesh):
+    fast = mesh.shape["seq"] == SEQ
     return jax.shard_map(
-        shards,
+        pair_shards if fast else shards,
         mesh=mesh,
         in_specs=(
             P("groups", "seq", None),

time: 775 us -> 298 us (0.38)
  waiting for transfers between devices: 616 us -> 0 us
  Pallas kernels: 0 us -> 263 us
  matrix products: 69 us -> 25.7 us
  local copies, waits for them, and re-layouts: 37.4 us -> 4.49 us
  starting transfers between devices: 18.3 us -> 0 us
  other arithmetic: 16.6 us -> 1.96 us
  between operations: 14.5 us -> 0.74 us
    all_to_all x1 -> x0, waiting for transfers between devices: 383 us -> none  [shards(): lax.all_to_all(stacked, 'seq', split_axis=0, concat_axis=0, tiled=True)]
    pallas_call x0 -> x4, Pallas kernels: none -> 263 us  [the longest x1 86.1 us: reduce_grads(): pl.pallas_call(functools.partial(reduce_kernel, scale), out_shape=jax.Sha...]
    all_gather x2 -> x0, waiting for transfers between devices: 140 us -> none  [the longest x1 107 us: shards(): lax.all_gather(proj_weight, 'seq', axis=0, tiled=True)]
    ppermute x4 -> x0, waiting for transfers between devices: 91.8 us -> none  [from_behind(): return lax.ppermute(block, axis, route)]
    dot_general x12 -> x4, matrix products: 69 us -> 25.7 us  [the longest x1 10.8 us: pair_shards(): jnp.dot(earlier, full[2].T, preferred_element_type=F32)]
    another operation x1 -> x0, local copies, waits for them, and re-layouts: 34.4 us -> none  [shards(): stacked = jnp.stack(local_terms, axis=1)]
    ppermute x4 -> x0, starting transfers between devices: 12.9 us -> none  [from_behind(): return lax.ppermute(block, axis, route)]
    reduce_sum x1 -> x0, other arithmetic: 10.4 us -> none  [shards(): jnp.sum(received.reshape(devices, share, 4, received.shape[2]), axis=0)]
  transfers between devices with their start and end apart: 7 -> 0, of which waited for: 5 -> 0; matrix products, arithmetic and copies ran while one was open for 7% -> 0% of each run, Pallas kernels for 0% -> 0%
where the time goes in v1:
time: 298 us; the launch traced here: 296 us
  Pallas kernels  263 us (88%)
  matrix products  25.7 us (9%)
  local copies, waits for them, and re-layouts  4.49 us (2%)
    pallas_call x1, Pallas kernels, reduce_grads(): pl.pallas_call(functools.partial(reduce_kernel, scale), out_shape=jax.Sha...  86.1 us
    pallas_call x1, Pallas kernels, forward(): pl.pallas_call(forward_kernel, out_shape=(jax.ShapeDtypeStruct((m, hid),...  67 us
    pallas_call x1, Pallas kernels, gather(): pl.pallas_call(gather_kernel, out_shape=(jax.ShapeDtypeStruct((taps, shar...  62.5 us
    pallas_call x1, Pallas kernels, halo(): pl.pallas_call(halo_kernel, out_shape=(jax.ShapeDtypeStruct((m, hid), BF1...  47.3 us
    dot_general x1, matrix products, pair_shards(): jnp.dot(earlier, full[2].T, preferred_element_type=F32)  10.8 us
    dot_general x1, matrix products, pair_shards(): acted_grad = jnp.dot(later, full[0].T, preferred_element_type=F32)  6.31 us

profile of v1, /device:TPU:15, one launch (start us, length us, event | category | flops | bytes accessed | tf_op | source)
XLA Modules:
  0.0 295.8 jit_solution(7356943192107557412)
XLA Ops:
  0.6 2.0 pad_maximum_fusion.w_ref
  2.6 62.5 %gather_weights.1 = (bf16[4,1536,768]{2,1,0:T(8,128)(2,1)}, bf16[1024,1536]{1,0:T(8,128)(2,1)}) custom-call(bf16[4,96,768]{2,1,0:T(8,128)(2,1)} %pad_maximum_fusion.w_ref, bf16[1024,1536]{1,0:T(8,128)(2,1)} %bitcast.30), custom_call_target="tpu_custom_call" | custom-call | tf_op jit(solution)/shard_map/gather_weights/pallas_call | solution.py:205
  65.1 67.0 %forward_halo.1 = (bf16[1024,768]{1,0:T(8,128)(2,1)}, bf16[1024,768]{1,0:T(8,128)(2,1)}) custom-call(bf16[1024,1536]{1,0:T(8,128)(2,1)} %get-tuple-element.10.acted_ref, bf16[4,1536,768]{2,1,0:T(8,128)(2,1)} %get-tuple-element.11.w_ref, bf16[1024,1536]{1,0:T(8,128)(2,1)} %bitcast.25), custom_call_target="tpu_custom_call" | custom-call | tf_op jit(solution)/shard_map/forward_halo/pallas_call | solution.py:298
  132.2 47.3 %backward_halo.1 = (bf16[1024,768]{1,0:T(8,128)(2,1)}, bf16[1024,768]{1,0:T(8,128)(2,1)}) custom-call(bf16[1024,768]{1,0:T(8,128)(2,1)} %get-tuple-element.13.hg_ref), custom_call_target="tpu_custom_call" | custom-call | tf_op jit(solution)/shard_map/backward_halo/pallas_call | solution.py:384
  179.5 0.0 copy-start.5
  179.5 0.0 slice-start
  179.5 0.0 slice-start.1
  179.5 86.1 %reduce_grads.1 = f32[4,96,768]{2,1,0:T(8,128)} custom-call(bf16[1024,1536]{1,0:T(8,128)(2,1)} %get-tuple-element.10.acted_ref, bf16[1024,1536]{1,0:T(8,128)(2,1)} %bitcast.26, bf16[1024,768]{1,0:T(8,128)(2,1)} %get-tuple-element.14.later_ref, bf16[1024,768]{1,0:T(8,128)(2,1)} %get-tuple-element.13.hg_ref, bf16[1024,768]{1,0:T(8,128)(2,1)} %get-tuple-element.15.earlier_ref, ...), custom_call_target="tpu_custom_call" | custom-call | tf_op jit(solution)/shard_map/reduce_grads/pallas_call | solution.py:498
  265.6 2.1 slice_bitcast_fusion
  267.7 1.7 slice_bitcast_fusion.1
  269.4 0.0 copy-done.5
  269.4 0.0 slice-start.2
  269.4 0.0 copy-start.1
  269.4 6.3 %fusion.14 = f32[1024,1536]{1,0:T(8,128)} fusion(bf16[1024,768]{1,0:T(8,128)(2,1)S(1)} %copy-done.5, bf16[4,1536,768]{2,1,0:T(8,128)(2,1)} %get-tuple-element.11.w_ref), kind=kOutput, calls=%fused_computation.19 | convolution fusion | flops 2415919104 | bytes 10223616 | tf_op jit(solution)/shard_map/dot_general | solution.py:530
  275.7 0.0 slice-done
  275.7 0.0 slice-done.1
  275.7 0.0 slice-done.2
  275.7 0.0 copy-done.1
  275.8 0.0 copy-start
  275.8 0.0 copy-start.2
  275.8 0.0 copy-start.4
  275.8 4.6 %fusion.12 = f32[1024,1536]{1,0:T(8,128)} fusion(bf16[1024,768]{1,0:T(8,128)(2,1)S(1)} %copy-done.1, bf16[4,1536,768]{2,1,0:T(8,128)(2,1)S(1)} %bitcast.29), kind=kOutput, calls=%fused_computation.17 | convolution fusion | flops 2415919104 | bytes 10223616 | tf_op jit(solution)/shard_map/dot_general | solution.py:531
  280.4 0.0 copy-done
  280.4 0.0 copy-done.2
  280.4 0.6 copy-done.4
  281.0 0.0 copy-start.3
  281.0 10.8 %fusion.4 = bf16[1024,1536]{1,0:T(8,128)(2,1)} fusion(bf16[1024,1536]{1,0:T(8,128)(2,1)S(1)} %bitcast.31, f32[1024,1536]{1,0:T(8,128)} %fusion.14, f32[1024,1536]{1,0:T(8,128)} %fusion.12, bf16[1024,1536]{1,0:T(8,128)(2,1)S(1)} %bitcast.27, bf16[1024,768]{1,0:T(8,128)(2,1)S(1)} %copy-done.4, bf16[4,1536,768]{2,1,0:T(8,128)(2,1)S(1)} %bitcast.29), kind=kOutput, calls=%fused_computation.9 | convolution fusion | flops 2455240704 | bytes 25952256 | tf_op jit(solution)/shard_map/dot_general | solution.py:532
  291.8 0.0 copy-done.3
  291.8 4.0 %fusion.5 = bf16[1024,1536]{1,0:T(8,128)(2,1)} fusion(bf16[1024,1536]{1,0:T(8,128)(2,1)S(1)} %bitcast.32, bf16[1024,768]{1,0:T(8,128)(2,1)S(1)} %copy-done.3, bf16[4,1536,768]{2,1,0:T(8,128)(2,1)S(1)} %bitcast.29), kind=kOutput, calls=%fused_computation.10 | convolution fusion | flops 2420637696 | bytes 10223616 | tf_op jit(solution)/shard_map/dot_general | solution.py:528
  (1 shorter events, 0.0 us)
Async XLA Ops:
  179.5 89.9 %copy-start.5 = (bf16[1024,768]{1,0:T(8,128)(2,1)S(1)}, bf16[1024,768]{1,0:T(8,128)(2,1)}, u32[]{:S(2)}) copy-start(bf16[1024,768]{1,0:T(8,128)(2,1)} %get-tuple-element.14.later_ref) | copy-start | bytes 4718596
  179.5 96.2 %slice-start = ((s8[9437184]{0:T(1024)(128)(4,1)}), s8[4194304]{0:T(1024)(128)(4,1)S(1)}, s32[]{:S(2)}) async-start(s8[9437184]{0:T(1024)(128)(4,1)} %bitcast.28), calls=%async_computation | async-start | bytes 8388608
  179.5 96.2 %slice-start.1 = ((s8[9437184]{0:T(1024)(128)(4,1)}), s8[1048576]{0:T(1024)(128)(4,1)S(1)}, s32[]{:S(2)}) async-start(s8[9437184]{0:T(1024)(128)(4,1)} %bitcast.28), calls=%async_computation.1 | async-start | bytes 2097152
  269.4 6.3 %slice-start.2 = ((s8[9437184]{0:T(1024)(128)(4,1)}), s8[4194304]{0:T(1024)(128)(4,1)S(1)}, s32[]{:S(2)}) async-start(s8[9437184]{0:T(1024)(128)(4,1)} %bitcast.28), calls=%async_computation.2 | async-start | bytes 8388608
  269.4 6.3 %copy-start.1 = (bf16[1024,768]{1,0:T(8,128)(2,1)S(1)}, bf16[1024,768]{1,0:T(8,128)(2,1)}, u32[]{:S(2)}) copy-start(bf16[1024,768]{1,0:T(8,128)(2,1)} %get-tuple-element.13.hg_ref) | copy-start | bytes 4718596
  275.8 4.6 %copy-start = (bf16[2,512,1536]{2,1,0:T(8,128)(2,1)S(1)}, bf16[2,512,1536]{2,1,0:T(8,128)(2,1)}, u32[]{:S(2)}) copy-start(bf16[2,512,1536]{2,1,0:T(8,128)(2,1)} %param.7) | copy-start | bytes 9437188
  275.8 4.6 %copy-start.2 = (bf16[2,512,1536]{2,1,0:T(8,128)(2,1)S(1)}, bf16[2,512,1536]{2,1,0:T(8,128)(2,1)}, u32[]{:S(2)}) copy-start(bf16[2,512,1536]{2,1,0:T(8,128)(2,1)} %param.4) | copy-start | bytes 9437188
  275.8 5.2 %copy-start.4 = (bf16[1024,768]{1,0:T(8,128)(2,1)S(1)}, bf16[1024,768]{1,0:T(8,128)(2,1)}, u32[]{:S(2)}) copy-start(bf16[1024,768]{1,0:T(8,128)(2,1)} %get-tuple-element.15.earlier_ref) | copy-start | bytes 4718596
  281.0 10.8 %copy-start.3 = (bf16[1024,768]{1,0:T(8,128)(2,1)S(1)}, bf16[1024,768]{1,0:T(8,128)(2,1)}, u32[]{:S(2)}) copy-start(bf16[1024,768]{1,0:T(8,128)(2,1)} %get-tuple-element.12.gated_ref) | copy-start | bytes 4718596

commit v2 on v1

--- a/solution.py
+++ b/solution.py
@@ -307,213 +307,254 @@
     )(acted, w4, cot)
 
 
-def halo_kernel(hg_ref, later_ref, earlier_ref, from_x, from_z, zs, zr, xs, xr):
+ORDER = (2, 1, 3, 0)
+PASSES = ((1, 3), (0, 2))
+NT = (((1,), (1,)), ((), ()))
+TN = (((0,), (0,)), ((), ()))
+
+
+def backward_kernel(scale, hg_ref, acted_ref, cot_ref, gated_ref, x_hbm, w_hbm,
+                    grads_ref, outputs_hbm, input_grad_hbm,
+                    x_buf, w_buf, o_buf, g_buf, near, give, keep, got, acc,
+                    x_out, x_in, z_out, z_in, load, store,
+                    hzs, hzr, hxs, hxr, cs, cr, xs, xr, zs, zr, free):
     z, x, core = place()
+    share = grads_ref.shape[1]
+    zt = [lax.rem(z + d, 4) for d in range(4)]
+    across = index(z, 1 - x, core)
+    other = index(z, x, 1 - core)
     even = x == 0
     sends = jnp.logical_or(jnp.logical_and(even, z < 3), jnp.logical_and(x == 1, z > 0))
     takes = jnp.logical_or(jnp.logical_and(even, z > 0), jnp.logical_and(x == 1, z < 3))
-    step = 1 - 2 * x
-    ahead = index(lax.rem(z + step + 4, 4), x, core)
-    behind = index(lax.rem(z - step + 4, 4), x, core)
-    across = index(z, 1 - x, core)
-    greet([ahead, behind, across])
-    n = hg_ref.shape[0] // CHUNKS
+    ahead = index(lax.rem(z + (1 - 2 * x) + 4, 4), x, core)
+    w_load = pltpu.make_async_copy(w_hbm, w_buf, load.at[0])
+    x_load = pltpu.make_async_copy(x_hbm, x_buf, load.at[1])
+    w_load.start()
+    x_load.start()
+    greet([index(zt[d], x, core) for d in (1, 2, 3)] + [across, other])
+    wide = 4 * share
+    tile = 256
+    m, hid = hg_ref.shape
+    chans = acted_ref.shape[1]
+    n = m // CHUNKS
 
     def rows(i):
         return pl.ds(pl.multiple_of(i * n, n), n)
 
-    def x_copy(i):
-        return copy_to(hg_ref.at[rows(i), :], from_x.at[i], xs.at[i], xr.at[i], across)
-
-    def z_copy(i):
-        return copy_to(from_x.at[i], from_z.at[i], zs.at[i], zr.at[i], ahead)
-
-    def launch(i, carry):
-        x_copy(i).start()
-        return carry
-
-    lax.fori_loop(0, CHUNKS, launch, 0)
-
-    def onward(i, carry):
-        x_copy(i).wait_recv()
+    def halo_x(i):
+        return copy_to(hg_ref.at[rows(i), :], near.at[0, rows(i), :], hxs.at[i], hxr.at[i], across)
+
+    def halo_z(i):
+        return copy_to(near.at[0, rows(i), :], near.at[1, rows(i), :], hzs.at[i], hzr.at[i], ahead)
+
+    def core_copy(s):
+        return copy_to(give.at[s % 2], got.at[s % 2], cs.at[s], cr.at[s], other)
+
+    def x_copy(s):
+        return copy_to(x_out.at[s], x_in.at[s], xs.at[s], xr.at[s], across)
+
+    def z_copy(s):
+        j = s // 4 * 3 + s % 4
+        target = index(zt[ORDER[s % 4]], x, core)
+        return copy_to(z_out.at[j], z_in.at[j], zs.at[j], zr.at[j], target)
+
+    def onward(i):
+        halo_x(i).wait_recv()
 
         @pl.when(sends)
         def _():
-            z_copy(i).start()
-        return carry
-
-    lax.fori_loop(0, CHUNKS, onward, 0)
-
-    def finish(i, carry):
-        @pl.when(takes)
-        def _():
-            z_copy(i).wait_recv()
-
-        @pl.when(jnp.logical_not(takes))
-        def _():
-            from_z[i] = jnp.zeros(from_z.shape[1:], BF16)
-
-        @pl.when(even)
-        def _():
-            later_ref[rows(i), :] = from_x[i]
-            earlier_ref[rows(i), :] = from_z[i]
-
-        @pl.when(x == 1)
-        def _():
-            later_ref[rows(i), :] = from_z[i]
-            earlier_ref[rows(i), :] = from_x[i]
-        return carry
-
-    lax.fori_loop(0, CHUNKS, finish, 0)
-
-    def drain(i, carry):
-        x_copy(i).wait_send()
-
-        @pl.when(sends)
-        def _():
-            z_copy(i).wait_send()
-        return carry
-
-    lax.fori_loop(0, CHUNKS, drain, 0)
-
-
-def halo(hg):
-    m, hid = hg.shape
-    dma = pltpu.SemaphoreType.DMA
-    block = (CHUNKS, m // CHUNKS, hid)
-    return pl.pallas_call(
-        halo_kernel,
-        out_shape=(jax.ShapeDtypeStruct((m, hid), BF16),) * 2,
-        in_specs=[VMEM],
-        out_specs=(VMEM, VMEM),
-        scratch_shapes=[pltpu.VMEM(block, BF16)] * 2 + [dma((CHUNKS,))] * 4,
-        compiler_params=params(2),
-        name="backward_halo",
-    )(hg)
-
-
-ORDER = (2, 1, 3, 0)
-
-
-def reduce_kernel(scale, acted_ref, cot_ref, later_ref, hg_ref, earlier_ref, gated_ref, out_ref,
-                  give, keep, got, acc, x_out, x_in, z_out, z_in, cs, cr, xs, xr, zs, zr):
-    z, x, core = place()
-    share = out_ref.shape[1]
-    zt = [lax.rem(z + d, 4) for d in range(4)]
-    across = index(z, 1 - x, core)
-    other = index(z, x, 1 - core)
-    greet([index(zt[d], x, core) for d in (1, 2, 3)] + [across, other])
-    taps = (later_ref, hg_ref, earlier_ref, gated_ref)
-    wide = 4 * share
-    tile = 256
-    hid = hg_ref.shape[1]
-
-    def core_copy(s):
-        return copy_to(give.at[s % 2], got.at[s], cs.at[s], cr.at[s], other)
-
-    def x_copy(s):
-        return copy_to(x_out.at[s], x_in.at[s], xs.at[s], xr.at[s], across)
-
-    def z_copy(s):
-        return copy_to(z_out.at[s], z_in.at[s], zs.at[s], zr.at[s], index(zt[ORDER[s]], x, core))
+            halo_z(i).start()
 
     def compute(s):
-        cols = pl.ds(pl.multiple_of(zt[ORDER[s]] * wide, wide), wide)
-        for k in range(4):
+        if s >= 2:
+            core_copy(s - 2).wait_send()
+        cols = pl.ds(pl.multiple_of(zt[ORDER[s % 4]] * wide, wide), wide)
+        for j, k in enumerate(PASSES[s // 4]):
             left = cot_ref if k == 3 else acted_ref
 
-            def part(i, carry, k=k, left=left):
+            def part(i, carry, k=k, j=j, left=left):
                 t = pl.ds(pl.multiple_of(i * tile, tile), tile)
-                p = lax.dot_general(left[:, cols], taps[k][:, t], (((0,), (0,)), ((), ())),
-                                    preferred_element_type=F32)
+                if k == 3:
+                    right = gated_ref[:, t]
+                elif k == 1:
+                    right = hg_ref[:, t]
+                else:
+                    right = near[x if k == 0 else 1 - x, :, t]
+                p = lax.dot_general(left[:, cols], right, TN, preferred_element_type=F32)
                 for xx in range(2):
                     lo = p[2 * xx * share:(2 * xx + 1) * share]
                     hi = p[(2 * xx + 1) * share:(2 * xx + 2) * share]
-                    keep[s % 2, xx, k, :, t] = jnp.where(core == 0, lo, hi)
-                    give[s % 2, xx, k, :, t] = jnp.where(core == 0, hi, lo)
+                    keep[s % 2, xx, j, :, t] = jnp.where(core == 0, lo, hi)
+                    give[s % 2, xx, j, :, t] = jnp.where(core == 0, hi, lo)
                 return carry
 
             lax.fori_loop(0, hid // tile, part, 0)
+        if s >= 2:
+            pl.semaphore_wait(free, 1)
         core_copy(s).start()
 
     def to_across(s):
         core_copy(s).wait_recv()
 
-        def add(k, carry):
-            x_out[s, k] = (keep[s % 2, 1 - x, k] + got[s, 1 - x, k]).astype(BF16)
-            acc[s, k] = keep[s % 2, x, k] + got[s, x, k]
+        def add(j, carry):
+            x_out[s, j] = (keep[s % 2, 1 - x, j] + got[s % 2, 1 - x, j]).astype(BF16)
+            acc[s, j] = keep[s % 2, x, j] + got[s % 2, x, j]
             return carry
 
-        lax.fori_loop(0, 4, add, 0)
+        lax.fori_loop(0, 2, add, 0)
         x_copy(s).start()
+        if s < 6:
+            pl.semaphore_signal(free, inc=1, device_id={"seq": other}, device_id_type=MESH)
 
     def to_z(s):
         x_copy(s).wait_recv()
-
-        def add(k, carry):
-            z_out[s, k] = (acc[s, k] + x_in[s, k].astype(F32)).astype(BF16)
-            return carry
-
-        lax.fori_loop(0, 4, add, 0)
+        for j in range(2):
+            z_out[s // 4 * 3 + s % 4, j] = (acc[s, j] + x_in[s, j].astype(F32)).astype(BF16)
         z_copy(s).start()
+
+    span = 512
+
+    def out_store(i):
+        return pltpu.make_async_copy(o_buf.at[rows(i), :], outputs_hbm.at[rows(i), :], store.at[i])
+
+    def grad_store(i):
+        return pltpu.make_async_copy(
+            g_buf.at[rows(i), :], input_grad_hbm.at[rows(i), :], store.at[CHUNKS + i]
+        )
+
+    def project(i, carry):
+        def part(j, c):
+            t = pl.ds(pl.multiple_of(j * span, span), span)
+            p = lax.dot_general(gated_ref[rows(i), :], w_buf[3, t, :], NT, preferred_element_type=F32)
+            o_buf[rows(i), t] = (x_buf[rows(i), t].astype(F32) + p).astype(BF16)
+            return c
+
+        lax.fori_loop(0, chans // span, part, 0)
+        out_store(i).start()
+        return carry
+
+    def spread(i, carry):
+        def part(j, c):
+            t = pl.ds(pl.multiple_of(j * span, span), span)
+            p = lax.dot_general(hg_ref[rows(i), :], w_buf[1, t, :], NT, preferred_element_type=F32)
+            p += lax.dot_general(near[x, rows(i), :], w_buf[0, t, :], NT, preferred_element_type=F32)
+            p += lax.dot_general(near[1 - x, rows(i), :], w_buf[2, t, :], NT, preferred_element_type=F32)
+            slope = gelu_parts(x_buf[rows(i), t].astype(F32))[1]
+            g_buf[rows(i), t] = (cot_ref[rows(i), t].astype(F32) + p * slope).astype(BF16)
+            return c
+
+        lax.fori_loop(0, chans // span, part, 0)
+        grad_store(i).start()
+        return carry
+
+    for i in range(CHUNKS):
+        halo_x(i).start()
+
+    @pl.when(jnp.logical_not(takes))
+    def _():
+        near[1] = jnp.zeros((m, hid), BF16)
 
     compute(0)
     compute(1)
+    onward(0)
     to_across(0)
-    core_copy(0).wait_send()
     compute(2)
+    onward(1)
     to_across(1)
-    core_copy(1).wait_send()
     compute(3)
+    onward(2)
     to_across(2)
     to_z(0)
+    onward(3)
     to_across(3)
+    w_load.wait()
+    x_load.wait()
+    lax.fori_loop(0, CHUNKS, project, 0)
     to_z(1)
     to_z(2)
-    x_copy(3).wait_recv()
-    for s in range(3):
-        z_copy(s).wait_recv()
-
-    def total(k, carry):
-        own = acc[3, k] + x_in[3, k].astype(F32)
-        for s in range(3):
-            own = own + z_in[s, k].astype(F32)
-        out_ref[k] = own * scale
-        return carry
-
-    lax.fori_loop(0, 4, total, 0)
-    core_copy(2).wait_send()
-    core_copy(3).wait_send()
-    for s in range(4):
+
+    @pl.when(takes)
+    def _():
+        for i in range(CHUNKS):
+            halo_z(i).wait_recv()
+
+    compute(4)
+    compute(5)
+    to_across(4)
+    compute(6)
+    to_across(5)
+    compute(7)
+    to_across(6)
+    to_z(4)
+    to_across(7)
+    lax.fori_loop(0, 2, spread, 0)
+    to_z(5)
+    lax.fori_loop(2, CHUNKS, spread, 0)
+    to_z(6)
+    for s in (3, 7):
+        x_copy(s).wait_recv()
+        for j in range(s // 4 * 3, s // 4 * 3 + 3):
+            z_copy(s // 4 * 4 + j % 3).wait_recv()
+        for j in range(2):
+            own = acc[s, j] + x_in[s, j].astype(F32)
+            for i in range(s // 4 * 3, s // 4 * 3 + 3):
+                own = own + z_in[i, j].astype(F32)
+            grads_ref[PASSES[s // 4][j]] = own * scale
+    for i in range(CHUNKS):
+        out_store(i).wait()
+        grad_store(i).wait()
+        halo_x(i).wait_send()
+
+    @pl.when(sends)
+    def _():
+        for i in range(CHUNKS):
+            halo_z(i).wait_send()
+
+    core_copy(6).wait_send()
+    core_copy(7).wait_send()
+    for s in range(8):
         x_copy(s).wait_send()
-    for s in range(3):
-        z_copy(s).wait_send()
-
-
-def reduce_grads(scale, acted, cot, later, hg, earlier, gated):
-    chans, hid = acted.shape[1], hg.shape[1]
+        if s % 4 < 3:
+            z_copy(s).wait_send()
+
+
+def backward(scale, hg, acted, cot, gated, rows, full):
+    m, hid = hg.shape
+    chans = acted.shape[1]
     share = chans // SEQ
     dma = pltpu.SemaphoreType.DMA
-    pair = (2, 4, share, hid)
+    pair = (2, 2, share, hid)
     return pl.pallas_call(
-        functools.partial(reduce_kernel, scale),
-        out_shape=jax.ShapeDtypeStruct((4, share, hid), F32),
-        in_specs=[VMEM] * 6,
-        out_specs=VMEM,
+        functools.partial(backward_kernel, scale),
+        out_shape=(
+            jax.ShapeDtypeStruct((4, share, hid), F32),
+            jax.ShapeDtypeStruct((m, chans), BF16),
+            jax.ShapeDtypeStruct((m, chans), BF16),
+        ),
+        in_specs=[VMEM] * 4 + [HBM] * 2,
+        out_specs=(VMEM, HBM, HBM),
         scratch_shapes=[
+            pltpu.VMEM((m, chans), BF16),
+            pltpu.VMEM(full.shape, BF16),
+            pltpu.VMEM((m, chans), BF16),
+            pltpu.VMEM((m, chans), BF16),
+            pltpu.VMEM((2, m, hid), BF16),
             pltpu.VMEM((2,) + pair, F32),
             pltpu.VMEM((2,) + pair, F32),
-            pltpu.VMEM((4,) + pair, F32),
-            pltpu.VMEM((4, 4, share, hid), F32),
-            pltpu.VMEM((4, 4, share, hid), BF16),
-            pltpu.VMEM((4, 4, share, hid), BF16),
-            pltpu.VMEM((3, 4, share, hid), BF16),
-            pltpu.VMEM((3, 4, share, hid), BF16),
-            dma((4,)), dma((4,)), dma((4,)), dma((4,)), dma((3,)), dma((3,)),
+            pltpu.VMEM((2,) + pair, F32),
+            pltpu.VMEM((8, 2, share, hid), F32),
+            pltpu.VMEM((8, 2, share, hid), BF16),
+            pltpu.VMEM((8, 2, share, hid), BF16),
+            pltpu.VMEM((6, 2, share, hid), BF16),
+            pltpu.VMEM((6, 2, share, hid), BF16),
+            dma((2,)), dma((2 * CHUNKS,)),
+            dma((CHUNKS,)), dma((CHUNKS,)), dma((CHUNKS,)), dma((CHUNKS,)),
+            dma((8,)), dma((8,)), dma((8,)), dma((8,)), dma((6,)), dma((6,)),
+            pltpu.SemaphoreType.REGULAR,
         ],
-        compiler_params=params(3),
-        name="reduce_grads",
-    )(acted, cot, later, hg, earlier, gated)
+        compiler_params=params(2, 62),
+        name="backward_halo_and_reduce",
+    )(hg, acted, cot, gated, rows, full)
 
 
 def pair_shards(inputs, conv_weight, proj_weight, cotangent):
@@ -523,15 +564,7 @@
     cot = cotangent.reshape(-1, chans)
     full, acted = gather(jnp.concatenate([conv_weight, proj_weight[None]], axis=0), rows)
     gated, hg = forward(acted, full, cot)
-    later, earlier = halo(hg)
-    outputs = (
-        rows.astype(F32) + jnp.dot(gated, full[3].T, preferred_element_type=F32)
-    ).astype(BF16)
-    acted_grad = jnp.dot(later, full[0].T, preferred_element_type=F32)
-    acted_grad = acted_grad + jnp.dot(hg, full[1].T, preferred_element_type=F32)
-    acted_grad = acted_grad + jnp.dot(earlier, full[2].T, preferred_element_type=F32)
-    input_grad = (cot.astype(F32) + gelu_grad(rows.astype(F32), acted_grad)).astype(BF16)
-    grads = reduce_grads(scale, acted, cot, later, hg, earlier, gated)
+    grads, outputs, input_grad = backward(scale, hg, acted, cot, gated, rows, full)
     return (
         outputs.reshape(batch, local_len, chans),
         input_grad.reshape(batch, local_len, chans),

time: 298 us -> 257 us (0.86)
  matrix products: 25.7 us -> 0 us
  Pallas kernels: 263 us -> 241 us
  local copies, waits for them, and re-layouts: 4.49 us -> 9.4 us
    dot_general x4 -> x0, matrix products: 25.7 us -> none  [the longest x1 10.8 us: pair_shards(): jnp.dot(earlier, full[2].T, preferred_element_type=F32)]
    pallas_call x2 -> x1, Pallas kernels: 133 us -> 111 us  [backward(): pl.pallas_call(functools.partial(backward_kernel, scale), out_shape=(jax....]
    unnamed x18 -> x4, local copies, waits for them, and re-layouts: 0.66 us -> 5.57 us
where the time goes in v2:
time: 257 us; the launch traced here: 253 us
  Pallas kernels  241 us (94%)
  local copies, waits for them, and re-layouts  9.4 us (4%)
    pallas_call x1, Pallas kernels, backward(): pl.pallas_call(functools.partial(backward_kernel, scale), out_shape=(jax....  111 us
    pallas_call x1, Pallas kernels, forward(): pl.pallas_call(forward_kernel, out_shape=(jax.ShapeDtypeStruct((m, hid),...  67.1 us
    pallas_call x1, Pallas kernels, gather(): pl.pallas_call(gather_kernel, out_shape=(jax.ShapeDtypeStruct((taps, shar...  62.5 us
    unnamed x4, local copies, waits for them, and re-layouts  5.57 us

profile of v2, /device:TPU:15, one launch (start us, length us, event | category | flops | bytes accessed | tf_op | source)
XLA Modules:
  0.0 252.8 jit_solution(15853387846891754954)
XLA Ops:
  0.6 2.0 pad_maximum_fusion.w_ref
  2.6 62.5 %gather_weights.1 = (bf16[4,1536,768]{2,1,0:T(8,128)(2,1)}, bf16[1024,1536]{1,0:T(8,128)(2,1)}) custom-call(bf16[4,96,768]{2,1,0:T(8,128)(2,1)} %pad_maximum_fusion.w_ref, bf16[1024,1536]{1,0:T(8,128)(2,1)} %bitcast.9), custom_call_target="tpu_custom_call" | custom-call | tf_op jit(solution)/shard_map/gather_weights/pallas_call | solution.py:205
  65.1 67.1 %forward_halo.1 = (bf16[1024,768]{1,0:T(8,128)(2,1)}, bf16[1024,768]{1,0:T(8,128)(2,1)}) custom-call(bf16[1024,1536]{1,0:T(8,128)(2,1)} %get-tuple-element.11.acted_ref, bf16[4,1536,768]{2,1,0:T(8,128)(2,1)} %get-tuple-element.12.w_ref.w_hbm, bf16[1024,1536]{1,0:T(8,128)(2,1)} %bitcast.11), custom_call_target="tpu_custom_call" | custom-call | tf_op jit(solution)/shard_map/forward_halo/pallas_call | solution.py:298
  132.2 111.2 %backward_halo_and_reduce.1 = (f32[4,96,768]{2,1,0:T(8,128)}, bf16[1024,1536]{1,0:T(8,128)(2,1)}, bf16[1024,1536]{1,0:T(8,128)(2,1)}) custom-call(bf16[1024,768]{1,0:T(8,128)(2,1)} %get-tuple-element.13.hg_ref, bf16[1024,1536]{1,0:T(8,128)(2,1)} %get-tuple-element.11.acted_ref, bf16[1024,1536]{1,0:T(8,128)(2,1)} %bitcast.12, ...), custom_call_target="tpu_custom_call" | custom-call | tf_op jit(solution)/shard_map/backward_halo_and_reduce/pallas_call | solution.py:527
  243.4 1.7 slice_bitcast_fusion.1
  245.1 2.1 slice_bitcast_fusion
  247.2 0.0 copy-start
  247.2 3.9 %copy.10 = bf16[2,512,1536]{2,1,0:T(8,128)(2,1)} copy(bf16[2,512,1536]{2,1,0:T(8,128)(2,1)} %bitcast.14) | data formatting | bytes 6291456
  251.1 0.0 copy-done
  251.1 1.7 copy.11
Async XLA Ops:
  247.2 3.9 %copy-start = (bf16[1024,1536]{1,0:T(8,128)(2,1)S(1)}, bf16[1024,1536]{1,0:T(8,128)(2,1)}, u32[]{:S(2)}) copy-start(bf16[1024,1536]{1,0:T(8,128)(2,1)} %get-tuple-element.16) | copy-start | bytes 9437188

commit v3 on v2

--- a/solution.py
+++ b/solution.py
@@ -126,40 +126,105 @@
     )
 
 
-def gather_kernel(w_ref, x_ref, full_ref, acted_ref, own_sem, zs, zr, xs, xr, cs, cr):
+def forward_kernel(w_ref, x_ref, cot_ref, full_hbm, acted_ref, gated_ref, hg_ref,
+                   w_buf, out_a, in_a, out_s, in_s, part, gg, own_sem,
+                   zs0, zr0, xs0, xr0, cs0, cr0, zs1, zr1, xs1, xr1, cs1, cr1,
+                   ys, yr, fs, fr, hzs, hzr, hxs, hxr):
     z, x, core = place()
+    group = lax.axis_index("groups")
+    me = lax.axis_index("seq")
     share = w_ref.shape[1]
     zt = [lax.rem(z + d, 4) for d in range(4)]
     zf = [lax.rem(z + 4 - d, 4) for d in range(4)]
-
-    def rows(zz, xx, cc):
-        start = pl.multiple_of(index(zz, xx, cc) * share, share)
-        return full_ref.at[:, pl.ds(start, share), :]
-
-    greet([index(zt[d], x, core) for d in (1, 2, 3)]
-          + [index(z, 1 - x, core), index(z, x, 1 - core)])
-    mine = rows(z, x, core)
-    copies = []
-    for d in (1, 3, 2):
-        copies.append(copy_to(w_ref, mine, zs.at[d], zr.at[d], index(zt[d], x, core)))
-        copies[-1].start()
-    zc = dict(zip((1, 3, 2), copies))
-
-    def to_x(j, src):
-        c = copy_to(src, rows(zf[j], x, core), xs.at[j], xr.at[j], index(z, 1 - x, core))
-        c.start()
-        return c
-
-    def to_core(j, src, xx):
-        c = copy_to(src, rows(zf[j % 4], xx, core), cs.at[j], cr.at[j], index(z, x, 1 - core))
-        c.start()
-        return c
-
-    xc = {0: to_x(0, w_ref)}
-    cc = {0: to_core(0, w_ref, x)}
-    own = pltpu.make_async_copy(w_ref, mine, own_sem)
+    across = index(z, 1 - x, core)
+    other = index(z, x, 1 - core)
+    up = x == 1
+    sends = jnp.logical_or(jnp.logical_and(up, z < 3), jnp.logical_and(x == 0, z > 0))
+    takes = jnp.logical_or(jnp.logical_and(up, z > 0), jnp.logical_and(x == 0, z < 3))
+    ahead = index(lax.rem(z + (2 * x - 1) + 4, 4), x, core)
+
+    barrier = pltpu.get_barrier_semaphore()
+    for target in [index(zt[d], x, core) for d in (1, 2, 3)] + [across, other]:
+        pl.semaphore_signal(barrier, inc=1, device_id={"seq": target}, device_id_type=MESH)
+    pl.semaphore_signal(
+        barrier, inc=1, device_id={"groups": 1 - group, "seq": me}, device_id_type=MESH
+    )
+    pl.semaphore_wait(barrier, 6)
+
+    def slab(first, count, zz, xx):
+        start = pl.multiple_of(index(zz, xx, core) * share, share)
+        return w_buf.at[pl.ds(first, count), pl.ds(start, share), :]
+
+    own_tap = 2 + group
+    far_tap = 3 - group
+    passes = ((0, 2, zs0, zr0, xs0, xr0, cs0, cr0), (own_tap, 1, zs1, zr1, xs1, xr1, cs1, cr1))
+
+    def column(j):
+        return zf[j % 4], (x if j < 4 else 1 - x)
+
+    def z_copy(p, d):
+        first, count, send, recv = passes[p][:4]
+        return copy_to(w_ref.at[pl.ds(first, count)], slab(first, count, z, x),
+                       send.at[d], recv.at[d], index(zt[d], x, core))
+
+    def x_copy(p, j):
+        first, count, _, _, send, recv = passes[p][:6]
+        place_ = slab(first, count, zf[j], x)
+        return copy_to(w_ref.at[pl.ds(first, count)] if j == 0 else place_, place_,
+                       send.at[j], recv.at[j], across)
+
+    def core_copy(p, j):
+        first, count, _, _, _, _, send, recv = passes[p]
+        if j == 0:
+            return copy_to(w_ref.at[pl.ds(2 * p, 2)], slab(2 * p, 2, z, x),
+                           send.at[0], recv.at[0], other)
+        place_ = slab(first, count, *column(j))
+        return copy_to(place_, place_, send.at[j], recv.at[j], other)
+
+    def y_copy(j):
+        place_ = slab(own_tap, 1, *column(j))
+        return pltpu.make_async_remote_copy(
+            src_ref=place_, dst_ref=place_, send_sem=ys.at[j], recv_sem=yr.at[j],
+            device_id={"groups": 1 - group, "seq": me}, device_id_type=MESH,
+        )
+
+    def relay_copy(j):
+        place_ = slab(far_tap, 1, *column(j))
+        return copy_to(place_, place_, fs.at[j], fr.at[j], other)
+
+    def begin(p):
+        for d in (1, 3, 2):
+            z_copy(p, d).start()
+        x_copy(p, 0).start()
+        core_copy(p, 0).start()
+
+    def take_z(p, j):
+        z_copy(p, j).wait_recv()
+        x_copy(p, j).start()
+        core_copy(p, j).start()
+        if p == 1:
+            y_copy(j).start()
+
+    def take_x(p, j):
+        x_copy(p, j).wait_recv()
+        core_copy(p, 4 + j).start()
+        if p == 1:
+            y_copy(4 + j).start()
+
+    n = acted_ref.shape[0] // CHUNKS
+
+    def rows(i):
+        return pl.ds(pl.multiple_of(i * n, n), n)
+
+    def halo_z(i):
+        return copy_to(out_a.at[i], in_a.at[i], hzs.at[i], hzr.at[i], ahead)
+
+    def halo_x(i):
+        return copy_to(out_s.at[i], in_s.at[i], hxs.at[i], hxr.at[i], across)
+
+    begin(0)
+    own = pltpu.make_async_copy(w_ref, slab(0, 4, z, x), own_sem.at[0])
     own.start()
-
     tile = 64
 
     def act(i, carry):
@@ -170,107 +235,72 @@
         return carry
 
     lax.fori_loop(0, x_ref.shape[0] // tile, act, 0)
-
-    def take_z(j):
-        zc[j].wait_recv()
-        src = rows(zf[j], x, core)
-        xc[j] = to_x(j, src)
-        cc[j] = to_core(j, src, x)
-
-    def take_x(j):
-        xc[j].wait_recv()
-        cc[4 + j] = to_core(4 + j, rows(zf[j], 1 - x, core), 1 - x)
-
-    take_z(1)
-    take_z(3)
-    take_x(0)
-    take_z(2)
-    take_x(1)
-    take_x(3)
-    take_x(2)
+    take_z(0, 1)
+    take_z(0, 3)
+    take_x(0, 0)
+    take_z(0, 2)
+    begin(1)
+    take_x(0, 1)
+    take_x(0, 3)
+    take_x(0, 2)
+    own.wait()
     for j in range(8):
-        cc[j].wait_recv()
-    own.wait()
-    for j in (1, 2, 3):
-        zc[j].wait_send()
-    for j in range(4):
-        xc[j].wait_send()
-    for j in range(8):
-        cc[j].wait_send()
-
-
-def gather(w4, flat):
-    taps, share, hid = w4.shape
-    dma = pltpu.SemaphoreType.DMA
-    return pl.pallas_call(
-        gather_kernel,
-        out_shape=(
-            jax.ShapeDtypeStruct((taps, share * SEQ, hid), BF16),
-            jax.ShapeDtypeStruct(flat.shape, BF16),
-        ),
-        in_specs=[HBM, VMEM],
-        out_specs=(HBM, VMEM),
-        scratch_shapes=[dma, dma((4,)), dma((4,)), dma((4,)), dma((4,)), dma((8,)), dma((8,))],
-        compiler_params=params(0),
-        name="gather_weights",
-    )(w4, flat)
-
-
-def forward_kernel(acted_ref, w_ref, cot_ref, gated_ref, hg_ref,
-                   out_a, in_a, out_s, in_s, part, gg, zs, zr, xs, xr):
-    z, x, core = place()
-    up = x == 1
-    sends = jnp.logical_or(jnp.logical_and(up, z < 3), jnp.logical_and(x == 0, z > 0))
-    takes = jnp.logical_or(jnp.logical_and(up, z > 0), jnp.logical_and(x == 0, z < 3))
-    step = 2 * x - 1
-    ahead = index(lax.rem(z + step + 4, 4), x, core)
-    behind = index(lax.rem(z - step + 4, 4), x, core)
-    across = index(z, 1 - x, core)
-    greet([ahead, behind, across])
-    n = acted_ref.shape[0] // CHUNKS
-    tap_far = 2 - 2 * x
-    tap_near = 2 * x
-
-    def rows(i):
-        return pl.ds(pl.multiple_of(i * n, n), n)
-
-    def z_copy(i):
-        return copy_to(out_a.at[i], in_a.at[i], zs.at[i], zr.at[i], ahead)
-
-    def x_copy(i):
-        return copy_to(out_s.at[i], in_s.at[i], xs.at[i], xr.at[i], across)
+        core_copy(0, j).wait_recv()
 
     def far(i, carry):
-        out_a[i] = jnp.dot(acted_ref[rows(i), :], w_ref[tap_far], preferred_element_type=F32).astype(BF16)
+        out_a[i] = jnp.dot(acted_ref[rows(i), :], w_buf[1 - x], preferred_element_type=F32).astype(BF16)
 
         @pl.when(sends)
         def _():
-            z_copy(i).start()
+            halo_z(i).start()
         return carry
 
     lax.fori_loop(0, CHUNKS, far, 0)
+    take_z(1, 1)
+    take_z(1, 3)
+    take_x(1, 0)
 
     def near(i, carry):
-        part[i] = jnp.dot(acted_ref[rows(i), :], w_ref[tap_near], preferred_element_type=F32)
-        gg[i] = jnp.dot(cot_ref[rows(i), :], w_ref[3], preferred_element_type=F32)
+        part[i] = jnp.dot(acted_ref[rows(i), :], w_buf[x], preferred_element_type=F32)
         return carry
 
     lax.fori_loop(0, CHUNKS, near, 0)
-
-    def combine(i, carry):
+    take_z(1, 2)
+
+    def combine(i):
         @pl.when(takes)
         def _():
-            z_copy(i).wait_recv()
+            halo_z(i).wait_recv()
             part[i] = part[i] + in_a[i].astype(F32)
         out_s[i] = part[i].astype(BF16)
-        x_copy(i).start()
-        part[i] = jnp.dot(acted_ref[rows(i), :], w_ref[1], preferred_element_type=F32)
+        halo_x(i).start()
+
+    combine(0)
+    take_x(1, 1)
+    take_x(1, 3)
+    combine(1)
+    take_x(1, 2)
+    combine(2)
+    for j in (1, 3, 4, 2, 5, 7, 6):
+        y_copy(j).wait_recv()
+        relay_copy(j).start()
+    combine(3)
+    for j in range(8):
+        core_copy(1, j).wait_recv()
+    for j in range(1, 8):
+        relay_copy(j).wait_recv()
+    keep = pltpu.make_async_copy(w_buf, full_hbm, own_sem.at[1])
+    keep.start()
+
+    def middle(i, carry):
+        part[i] = jnp.dot(acted_ref[rows(i), :], w_buf[2], preferred_element_type=F32)
+        gg[i] = jnp.dot(cot_ref[rows(i), :], w_buf[3], preferred_element_type=F32)
         return carry
 
-    lax.fori_loop(0, CHUNKS, combine, 0)
+    lax.fori_loop(0, CHUNKS, middle, 0)
 
     def finish(i, carry):
-        x_copy(i).wait_recv()
+        halo_x(i).wait_recv()
         hidden = part[i] + in_s[i].astype(F32)
         value, slope = gelu_parts(hidden)
         gated_ref[rows(i), :] = value.astype(BF16)
@@ -278,33 +308,46 @@
         return carry
 
     lax.fori_loop(0, CHUNKS, finish, 0)
-
-    def drain(i, carry):
-        x_copy(i).wait_send()
-
-        @pl.when(sends)
-        def _():
-            z_copy(i).wait_send()
-        return carry
-
-    lax.fori_loop(0, CHUNKS, drain, 0)
-
-
-def forward(acted, w4, cot):
-    m = acted.shape[0]
-    hid = w4.shape[2]
+    for p in range(2):
+        for d in (1, 2, 3):
+            z_copy(p, d).wait_send()
+        for j in range(4):
+            x_copy(p, j).wait_send()
+        for j in range(8):
+            core_copy(p, j).wait_send()
+    for j in range(1, 8):
+        y_copy(j).wait_send()
+        relay_copy(j).wait_send()
+    for i in range(CHUNKS):
+        halo_x(i).wait_send()
+
+    @pl.when(sends)
+    def _():
+        for i in range(CHUNKS):
+            halo_z(i).wait_send()
+
+    keep.wait()
+
+
+def forward(w4, flat, cot):
+    taps, share, hid = w4.shape
+    m = flat.shape[0]
     dma = pltpu.SemaphoreType.DMA
     block = (CHUNKS, m // CHUNKS, hid)
+    full = jax.ShapeDtypeStruct((taps, share * SEQ, hid), BF16)
     return pl.pallas_call(
         forward_kernel,
-        out_shape=(jax.ShapeDtypeStruct((m, hid), BF16),) * 2,
+        out_shape=(full, jax.ShapeDtypeStruct(flat.shape, BF16))
+        + (jax.ShapeDtypeStruct((m, hid), BF16),) * 2,
         in_specs=[VMEM] * 3,
-        out_specs=(VMEM, VMEM),
-        scratch_shapes=[pltpu.VMEM(block, BF16)] * 4 + [pltpu.VMEM(block, F32)] * 2
-        + [dma((CHUNKS,))] * 4,
+        out_specs=(HBM, VMEM, VMEM, VMEM),
+        scratch_shapes=[pltpu.VMEM(full.shape, BF16)]
+        + [pltpu.VMEM(block, BF16)] * 4 + [pltpu.VMEM(block, F32)] * 2
+        + [dma((2,))] + ([dma((4,))] * 4 + [dma((8,))] * 2) * 2
+        + [dma((8,))] * 4 + [dma((CHUNKS,))] * 4,
         compiler_params=params(1),
-        name="forward_halo",
-    )(acted, w4, cot)
+        name="gather_and_forward_halo",
+    )(w4, flat, cot)
 
 
 ORDER = (2, 1, 3, 0)
@@ -436,9 +479,9 @@
     def spread(i, carry):
         def part(j, c):
             t = pl.ds(pl.multiple_of(j * span, span), span)
-            p = lax.dot_general(hg_ref[rows(i), :], w_buf[1, t, :], NT, preferred_element_type=F32)
+            p = lax.dot_general(hg_ref[rows(i), :], w_buf[2, t, :], NT, preferred_element_type=F32)
             p += lax.dot_general(near[x, rows(i), :], w_buf[0, t, :], NT, preferred_element_type=F32)
-            p += lax.dot_general(near[1 - x, rows(i), :], w_buf[2, t, :], NT, preferred_element_type=F32)
+            p += lax.dot_general(near[1 - x, rows(i), :], w_buf[1, t, :], NT, preferred_element_type=F32)
             slope = gelu_parts(x_buf[rows(i), t].astype(F32))[1]
             g_buf[rows(i), t] = (cot_ref[rows(i), t].astype(F32) + p * slope).astype(BF16)
             return c
@@ -562,8 +605,8 @@
     scale = 1.0 / float(batch * L) ** 0.5
     rows = inputs.reshape(-1, chans)
     cot = cotangent.reshape(-1, chans)
-    full, acted = gather(jnp.concatenate([conv_weight, proj_weight[None]], axis=0), rows)
-    gated, hg = forward(acted, full, cot)
+    w4 = jnp.stack([conv_weight[0], conv_weight[2], conv_weight[1], proj_weight])
+    full, acted, gated, hg = forward(w4, rows, cot)
     grads, outputs, input_grad = backward(scale, hg, acted, cot, gated, rows, full)
     return (
         outputs.reshape(batch, local_len, chans),

time: 257 us -> 222 us (0.86)
  Pallas kernels: 241 us -> 206 us
    pallas_call x2 -> x1, Pallas kernels: 130 us -> 93.7 us  [forward(): pl.pallas_call(forward_kernel, out_shape=(full, jax.ShapeDtypeStruct(flat...]
where the time goes in v3:
time: 222 us; the launch traced here: 219 us
  Pallas kernels  206 us (93%)
  local copies, waits for them, and re-layouts  10.5 us (5%)
    pallas_call x1, Pallas kernels, backward(): pl.pallas_call(functools.partial(backward_kernel, scale), out_shape=(jax....  113 us
    pallas_call x1, Pallas kernels, forward(): pl.pallas_call(forward_kernel, out_shape=(full, jax.ShapeDtypeStruct(flat...  93.7 us
    unnamed x4, local copies, waits for them, and re-layouts  5.57 us

profile of v3, /device:TPU:15, one launch (start us, length us, event | category | flops | bytes accessed | tf_op | source)
XLA Modules:
  0.0 219.4 jit_solution(7948890460689855139)
XLA Ops:
  0.6 1.1 fusion
  1.7 1.8 pad_maximum_fusion.w_ref
  3.5 93.7 %gather_and_forward_halo.1 = (bf16[4,1536,768]{2,1,0:T(8,128)(2,1)}, bf16[1024,1536]{1,0:T(8,128)(2,1)}, bf16[1024,768]{1,0:T(8,128)(2,1)}, bf16[1024,768]{1,0:T(8,128)(2,1)}) custom-call(bf16[4,96,768]{2,1,0:T(8,128)(2,1)} %pad_maximum_fusion.w_ref, bf16[1024,1536]{1,0:T(8,128)(2,1)} %bitcast.9, bf16[1024,1536]{1,0:T(8,128)(2,1)} %bitcast.11), custom_call_target="tpu_custom_call" | custom-call | tf_op jit(solution)/shard_map/gather_and_forward_halo/pallas_call | solution.py:338
  97.2 112.7 %backward_halo_and_reduce.1 = (f32[4,96,768]{2,1,0:T(8,128)}, bf16[1024,1536]{1,0:T(8,128)(2,1)}, bf16[1024,1536]{1,0:T(8,128)(2,1)}) custom-call(bf16[1024,768]{1,0:T(8,128)(2,1)} %get-tuple-element.11.hg_ref, bf16[1024,1536]{1,0:T(8,128)(2,1)} %get-tuple-element.12.acted_ref, bf16[1024,1536]{1,0:T(8,128)(2,1)} %bitcast.12, ...), custom_call_target="tpu_custom_call" | custom-call | tf_op jit(solution)/shard_map/backward_halo_and_reduce/pallas_call | solution.py:570
  209.9 1.7 slice_bitcast_fusion.1
  211.6 2.1 slice_bitcast_fusion
  213.8 0.0 copy-start
  213.8 3.9 %copy.10 = bf16[2,512,1536]{2,1,0:T(8,128)(2,1)} copy(bf16[2,512,1536]{2,1,0:T(8,128)(2,1)} %bitcast.14) | data formatting | bytes 6291456
  217.7 0.0 copy-done
  217.7 1.7 copy.11
Async XLA Ops:
  213.8 3.9 %copy-start = (bf16[1024,1536]{1,0:T(8,128)(2,1)S(1)}, bf16[1024,1536]{1,0:T(8,128)(2,1)}, u32[]{:S(2)}) copy-start(bf16[1024,1536]{1,0:T(8,128)(2,1)} %get-tuple-element.16) | copy-start | bytes 9437188

commit v4 on v3

--- a/solution.py
+++ b/solution.py
@@ -87,6 +87,7 @@
 HBM = pl.BlockSpec(memory_space=pl.ANY)
 SEQ = 16
 CHUNKS = 4
+HALO = 8
 COEF = 0.7978845608028654
 CUBE = 0.044715
 
@@ -126,14 +127,14 @@
     )
 
 
-def forward_kernel(w_ref, x_ref, cot_ref, full_hbm, acted_ref, gated_ref, hg_ref,
-                   w_buf, out_a, in_a, out_s, in_s, part, gg, own_sem,
+def forward_kernel(conv_hbm, proj_hbm, x_hbm, cot_hbm, full_hbm, acted_hbm, gated_ref, hg_ref,
+                   w_buf, x_ref, cot_ref, acted_ref, out_a, in_a, out_s, in_s, part, gg, own_sem,
                    zs0, zr0, xs0, xr0, cs0, cr0, zs1, zr1, xs1, xr1, cs1, cr1,
                    ys, yr, fs, fr, hzs, hzr, hxs, hxr):
     z, x, core = place()
     group = lax.axis_index("groups")
     me = lax.axis_index("seq")
-    share = w_ref.shape[1]
+    share = proj_hbm.shape[0]
     zt = [lax.rem(z + d, 4) for d in range(4)]
     zf = [lax.rem(z + 4 - d, 4) for d in range(4)]
     across = index(z, 1 - x, core)
@@ -143,6 +144,18 @@
     takes = jnp.logical_or(jnp.logical_and(up, z > 0), jnp.logical_and(x == 0, z < 3))
     ahead = index(lax.rem(z + (2 * x - 1) + 4, 4), x, core)
 
+    mine = pl.ds(pl.multiple_of(me * share, share), share)
+    loads = [
+        pltpu.make_async_copy(conv_hbm.at[tap], w_buf.at[slot, mine, :], own_sem.at[slot])
+        for slot, tap in enumerate((0, 2, 1))
+    ]
+    loads.append(pltpu.make_async_copy(proj_hbm, w_buf.at[3, mine, :], own_sem.at[3]))
+    x_load = pltpu.make_async_copy(x_hbm, x_ref, own_sem.at[4])
+    cot_load = pltpu.make_async_copy(cot_hbm, cot_ref, own_sem.at[5])
+    for load in loads:
+        load.start()
+    x_load.start()
+    cot_load.start()
     barrier = pltpu.get_barrier_semaphore()
     for target in [index(zt[d], x, core) for d in (1, 2, 3)] + [across, other]:
         pl.semaphore_signal(barrier, inc=1, device_id={"seq": target}, device_id_type=MESH)
@@ -164,19 +177,19 @@
 
     def z_copy(p, d):
         first, count, send, recv = passes[p][:4]
-        return copy_to(w_ref.at[pl.ds(first, count)], slab(first, count, z, x),
+        return copy_to(slab(first, count, z, x), slab(first, count, z, x),
                        send.at[d], recv.at[d], index(zt[d], x, core))
 
     def x_copy(p, j):
         first, count, _, _, send, recv = passes[p][:6]
         place_ = slab(first, count, zf[j], x)
-        return copy_to(w_ref.at[pl.ds(first, count)] if j == 0 else place_, place_,
+        return copy_to(place_, place_,
                        send.at[j], recv.at[j], across)
 
     def core_copy(p, j):
         first, count, _, _, _, _, send, recv = passes[p]
         if j == 0:
-            return copy_to(w_ref.at[pl.ds(2 * p, 2)], slab(2 * p, 2, z, x),
+            return copy_to(slab(2 * p, 2, z, x), slab(2 * p, 2, z, x),
                            send.at[0], recv.at[0], other)
         place_ = slab(first, count, *column(j))
         return copy_to(place_, place_, send.at[j], recv.at[j], other)
@@ -222,9 +235,10 @@
     def halo_x(i):
         return copy_to(out_s.at[i], in_s.at[i], hxs.at[i], hxr.at[i], across)
 
+    for load in loads:
+        load.wait()
     begin(0)
-    own = pltpu.make_async_copy(w_ref, slab(0, 4, z, x), own_sem.at[0])
-    own.start()
+    x_load.wait()
     tile = 64
 
     def act(i, carry):
@@ -235,6 +249,8 @@
         return carry
 
     lax.fori_loop(0, x_ref.shape[0] // tile, act, 0)
+    acted_store = pltpu.make_async_copy(acted_ref, acted_hbm, own_sem.at[6])
+    acted_store.start()
     take_z(0, 1)
     take_z(0, 3)
     take_x(0, 0)
@@ -243,7 +259,7 @@
     take_x(0, 1)
     take_x(0, 3)
     take_x(0, 2)
-    own.wait()
+    cot_load.wait()
     for j in range(8):
         core_copy(0, j).wait_recv()
 
@@ -289,7 +305,7 @@
         core_copy(1, j).wait_recv()
     for j in range(1, 8):
         relay_copy(j).wait_recv()
-    keep = pltpu.make_async_copy(w_buf, full_hbm, own_sem.at[1])
+    keep = pltpu.make_async_copy(w_buf, full_hbm, own_sem.at[7])
     keep.start()
 
     def middle(i, carry):
@@ -327,10 +343,11 @@
             halo_z(i).wait_send()
 
     keep.wait()
-
-
-def forward(w4, flat, cot):
-    taps, share, hid = w4.shape
+    acted_store.wait()
+
+
+def forward(conv_weight, proj_weight, flat, cot):
+    taps, share, hid = 4, proj_weight.shape[0], proj_weight.shape[1]
     m = flat.shape[0]
     dma = pltpu.SemaphoreType.DMA
     block = (CHUNKS, m // CHUNKS, hid)
@@ -339,15 +356,15 @@
         forward_kernel,
         out_shape=(full, jax.ShapeDtypeStruct(flat.shape, BF16))
         + (jax.ShapeDtypeStruct((m, hid), BF16),) * 2,
-        in_specs=[VMEM] * 3,
-        out_specs=(HBM, VMEM, VMEM, VMEM),
-        scratch_shapes=[pltpu.VMEM(full.shape, BF16)]
+        in_specs=[HBM] * 4,
+        out_specs=(HBM, HBM, VMEM, VMEM),
+        scratch_shapes=[pltpu.VMEM(full.shape, BF16)] + [pltpu.VMEM(flat.shape, BF16)] * 3
         + [pltpu.VMEM(block, BF16)] * 4 + [pltpu.VMEM(block, F32)] * 2
-        + [dma((2,))] + ([dma((4,))] * 4 + [dma((8,))] * 2) * 2
+        + [dma((8,))] + ([dma((4,))] * 4 + [dma((8,))] * 2) * 2
         + [dma((8,))] * 4 + [dma((CHUNKS,))] * 4,
         compiler_params=params(1),
         name="gather_and_forward_halo",
-    )(w4, flat, cot)
+    )(conv_weight, proj_weight, flat, cot)
 
 
 ORDER = (2, 1, 3, 0)
@@ -356,9 +373,9 @@
 TN = (((0,), (0,)), ((), ()))
 
 
-def backward_kernel(scale, hg_ref, acted_ref, cot_ref, gated_ref, x_hbm, w_hbm,
+def backward_kernel(scale, hg_ref, acted_hbm, cot_hbm, gated_hbm, x_hbm, w_hbm,
                     grads_ref, outputs_hbm, input_grad_hbm,
-                    x_buf, w_buf, o_buf, g_buf, near, give, keep, got, acc,
+                    acted_ref, cot_ref, gated_ref, x_buf, w_buf, o_buf, g_buf, near, give, keep, got, acc,
                     x_out, x_in, z_out, z_in, load, store,
                     hzs, hzr, hxs, hxr, cs, cr, xs, xr, zs, zr, free):
     z, x, core = place()
@@ -372,6 +389,14 @@
     ahead = index(lax.rem(z + (1 - 2 * x) + 4, 4), x, core)
     w_load = pltpu.make_async_copy(w_hbm, w_buf, load.at[0])
     x_load = pltpu.make_async_copy(x_hbm, x_buf, load.at[1])
+    early = [
+        pltpu.make_async_copy(src, dst, load.at[2 + i])
+        for i, (src, dst) in enumerate(
+            ((acted_hbm, acted_ref), (cot_hbm, cot_ref), (gated_hbm, gated_ref))
+        )
+    ]
+    for copy in early:
+        copy.start()
     w_load.start()
     x_load.start()
     greet([index(zt[d], x, core) for d in (1, 2, 3)] + [across, other])
@@ -384,11 +409,16 @@
     def rows(i):
         return pl.ds(pl.multiple_of(i * n, n), n)
 
+    half = m // HALO
+
+    def piece(i):
+        return pl.ds(i * half, half)
+
     def halo_x(i):
-        return copy_to(hg_ref.at[rows(i), :], near.at[0, rows(i), :], hxs.at[i], hxr.at[i], across)
+        return copy_to(hg_ref.at[piece(i), :], near.at[0, piece(i), :], hxs.at[i], hxr.at[i], across)
 
     def halo_z(i):
-        return copy_to(near.at[0, rows(i), :], near.at[1, rows(i), :], hzs.at[i], hzr.at[i], ahead)
+        return copy_to(near.at[0, piece(i), :], near.at[1, piece(i), :], hzs.at[i], hzr.at[i], ahead)
 
     def core_copy(s):
         return copy_to(give.at[s % 2], got.at[s % 2], cs.at[s], cr.at[s], other)
@@ -490,46 +520,53 @@
         grad_store(i).start()
         return carry
 
-    for i in range(CHUNKS):
+    for i in range(HALO):
         halo_x(i).start()
 
     @pl.when(jnp.logical_not(takes))
     def _():
         near[1] = jnp.zeros((m, hid), BF16)
 
+    for copy in early:
+        copy.wait()
     compute(0)
     compute(1)
     onward(0)
+    onward(1)
+    onward(2)
+    onward(3)
+    w_load.wait()
+    x_load.wait()
+    lax.fori_loop(0, 2, project, 0)
+    onward(4)
+    onward(5)
     to_across(0)
     compute(2)
-    onward(1)
+    onward(6)
+    onward(7)
     to_across(1)
     compute(3)
-    onward(2)
     to_across(2)
+    to_across(3)
+    lax.fori_loop(2, CHUNKS, project, 0)
     to_z(0)
-    onward(3)
-    to_across(3)
-    w_load.wait()
-    x_load.wait()
-    lax.fori_loop(0, CHUNKS, project, 0)
-    to_z(1)
-    to_z(2)
 
     @pl.when(takes)
     def _():
-        for i in range(CHUNKS):
+        for i in range(HALO):
             halo_z(i).wait_recv()
 
     compute(4)
+    to_z(1)
     compute(5)
     to_across(4)
+    to_z(2)
     compute(6)
     to_across(5)
     compute(7)
     to_across(6)
+    to_across(7)
     to_z(4)
-    to_across(7)
     lax.fori_loop(0, 2, spread, 0)
     to_z(5)
     lax.fori_loop(2, CHUNKS, spread, 0)
@@ -546,11 +583,12 @@
     for i in range(CHUNKS):
         out_store(i).wait()
         grad_store(i).wait()
+    for i in range(HALO):
         halo_x(i).wait_send()
 
     @pl.when(sends)
     def _():
-        for i in range(CHUNKS):
+        for i in range(HALO):
             halo_z(i).wait_send()
 
     core_copy(6).wait_send()
@@ -574,9 +612,12 @@
             jax.ShapeDtypeStruct((m, chans), BF16),
             jax.ShapeDtypeStruct((m, chans), BF16),
         ),
-        in_specs=[VMEM] * 4 + [HBM] * 2,
+        in_specs=[VMEM] + [HBM] * 5,
         out_specs=(VMEM, HBM, HBM),
         scratch_shapes=[
+            pltpu.VMEM((m, chans), BF16),
+            pltpu.VMEM((m, chans), BF16),
+            pltpu.VMEM((m, hid), BF16),
             pltpu.VMEM((m, chans), BF16),
             pltpu.VMEM(full.shape, BF16),
             pltpu.VMEM((m, chans), BF16),
@@ -590,8 +631,8 @@
             pltpu.VMEM((8, 2, share, hid), BF16),
             pltpu.VMEM((6, 2, share, hid), BF16),
             pltpu.VMEM((6, 2, share, hid), BF16),
-            dma((2,)), dma((2 * CHUNKS,)),
-            dma((CHUNKS,)), dma((CHUNKS,)), dma((CHUNKS,)), dma((CHUNKS,)),
+            dma((5,)), dma((2 * CHUNKS,)),
+            dma((HALO,)), dma((HALO,)), dma((HALO,)), dma((HALO,)),
             dma((8,)), dma((8,)), dma((8,)), dma((8,)), dma((6,)), dma((6,)),
             pltpu.SemaphoreType.REGULAR,
         ],
@@ -605,8 +646,7 @@
     scale = 1.0 / float(batch * L) ** 0.5
     rows = inputs.reshape(-1, chans)
     cot = cotangent.reshape(-1, chans)
-    w4 = jnp.stack([conv_weight[0], conv_weight[2], conv_weight[1], proj_weight])
-    full, acted, gated, hg = forward(w4, rows, cot)
+    full, acted, gated, hg = forward(conv_weight, proj_weight, rows, cot)
     grads, outputs, input_grad = backward(scale, hg, acted, cot, gated, rows, full)
     return (
         outputs.reshape(batch, local_len, chans),

time: 222 us -> 203 us (0.914)
  Pallas kernels: 206 us -> 192 us
    pallas_call x1, Pallas kernels: 113 us -> 102 us  [backward(): pl.pallas_call(functools.partial(backward_kernel, scale), out_shape=(jax....]
    pallas_call x1, Pallas kernels: 93.7 us -> 89.9 us  [forward(): pl.pallas_call(forward_kernel, out_shape=(full, jax.ShapeDtypeStruct(flat...]
where the time goes in v4:
time: 203 us; the launch traced here: 202 us
  Pallas kernels  192 us (95%)
  local copies, waits for them, and re-layouts  9.4 us (5%)
    pallas_call x1, Pallas kernels, backward(): pl.pallas_call(functools.partial(backward_kernel, scale), out_shape=(jax....  102 us
    pallas_call x1, Pallas kernels, forward(): pl.pallas_call(forward_kernel, out_shape=(full, jax.ShapeDtypeStruct(flat...  89.9 us
    unnamed x4, local copies, waits for them, and re-layouts  5.57 us

profile of v4, /device:TPU:15, one launch (start us, length us, event | category | flops | bytes accessed | tf_op | source)
XLA Modules:
  0.0 201.6 jit_solution(3567359171942668647)
XLA Ops:
  0.6 89.9 %gather_and_forward_halo.1 = (bf16[4,1536,768]{2,1,0:T(8,128)(2,1)}, bf16[1024,1536]{1,0:T(8,128)(2,1)}, bf16[1024,768]{1,0:T(8,128)(2,1)}, bf16[1024,768]{1,0:T(8,128)(2,1)}) custom-call(bf16[3,96,768]{2,1,0:T(8,128)(2,1)} %conv_hbm.1, bf16[96,768]{1,0:T(8,128)(2,1)} %proj_hbm.1, bf16[1024,1536]{1,0:T(8,128)(2,1)} %bitcast.8, bf16[1024,1536]{1,0:T(8,128)(2,1)} %bitcast.10), custom_call_target="tpu_custom_call" | custom-call | tf_op jit(solution)/shard_map/gather_and_forward_halo/pallas_call | solution.py:355
  90.5 101.7 %backward_halo_and_reduce.1 = (f32[4,96,768]{2,1,0:T(8,128)}, bf16[1024,1536]{1,0:T(8,128)(2,1)}, bf16[1024,1536]{1,0:T(8,128)(2,1)}) custom-call(bf16[1024,768]{1,0:T(8,128)(2,1)} %get-tuple-element.11.hg_ref, bf16[1024,1536]{1,0:T(8,128)(2,1)} %get-tuple-element.12.acted_hbm, bf16[1024,1536]{1,0:T(8,128)(2,1)} %bitcast.11, ...), custom_call_target="tpu_custom_call" | custom-call | tf_op jit(solution)/shard_map/backward_halo_and_reduce/pallas_call | solution.py:608
  192.2 1.7 slice_bitcast_fusion.1
  193.9 2.1 %slice_bitcast_fusion = f32[96,3,768]{2,0,1:T(8,128)} fusion(f32[4,96,768]{2,1,0:T(8,128)} %get-tuple-element.17), kind=kLoop, calls=%fused_computation | loop fusion | bytes 1769472 | tf_op jit(solution)/shard_map/transpose | solution.py:654
  196.1 0.0 copy-start
  196.1 3.9 %copy.10 = bf16[2,512,1536]{2,1,0:T(8,128)(2,1)} copy(bf16[2,512,1536]{2,1,0:T(8,128)(2,1)} %bitcast.13) | data formatting | bytes 6291456
  200.0 0.0 copy-done
  200.0 1.7 copy.11
Async XLA Ops:
  196.1 3.9 %copy-start = (bf16[1024,1536]{1,0:T(8,128)(2,1)S(1)}, bf16[1024,1536]{1,0:T(8,128)(2,1)}, u32[]{:S(2)}) copy-start(bf16[1024,1536]{1,0:T(8,128)(2,1)} %get-tuple-element.16) | copy-start | bytes 9437188

commit v5 on v4

--- a/solution.py
+++ b/solution.py
@@ -300,7 +300,6 @@
     for j in (1, 3, 4, 2, 5, 7, 6):
         y_copy(j).wait_recv()
         relay_copy(j).start()
-    combine(3)
     for j in range(8):
         core_copy(1, j).wait_recv()
     for j in range(1, 8):
@@ -313,7 +312,9 @@
         gg[i] = jnp.dot(cot_ref[rows(i), :], w_buf[3], preferred_element_type=F32)
         return carry
 
-    lax.fori_loop(0, CHUNKS, middle, 0)
+    lax.fori_loop(0, CHUNKS - 1, middle, 0)
+    combine(CHUNKS - 1)
+    lax.fori_loop(CHUNKS - 1, CHUNKS, middle, 0)
 
     def finish(i, carry):
         halo_x(i).wait_recv()

time: 203 us -> 203 us (level)
  no operation moved by 1% of the time
where the time goes in v5:
time: 203 us; the launch traced here: 202 us
  Pallas kernels  192 us (95%)
  local copies, waits for them, and re-layouts  9.4 us (5%)
    pallas_call x1, Pallas kernels, backward(): pl.pallas_call(functools.partial(backward_kernel, scale), out_shape=(jax....  102 us
    pallas_call x1, Pallas kernels, forward(): pl.pallas_call(forward_kernel, out_shape=(full, jax.ShapeDtypeStruct(flat...  89.9 us
    unnamed x4, local copies, waits for them, and re-layouts  5.57 us

profile of v5, /device:TPU:15, one launch (start us, length us, event | category | flops | bytes accessed | tf_op | source)
XLA Modules:
  0.0 201.6 jit_solution(3157498198324099888)
XLA Ops:
  0.6 89.9 %gather_and_forward_halo.1 = (bf16[4,1536,768]{2,1,0:T(8,128)(2,1)}, bf16[1024,1536]{1,0:T(8,128)(2,1)}, bf16[1024,768]{1,0:T(8,128)(2,1)}, bf16[1024,768]{1,0:T(8,128)(2,1)}) custom-call(bf16[3,96,768]{2,1,0:T(8,128)(2,1)} %conv_hbm.1, bf16[96,768]{1,0:T(8,128)(2,1)} %proj_hbm.1, bf16[1024,1536]{1,0:T(8,128)(2,1)} %bitcast.8, bf16[1024,1536]{1,0:T(8,128)(2,1)} %bitcast.10), custom_call_target="tpu_custom_call" | custom-call | tf_op jit(solution)/shard_map/gather_and_forward_halo/pallas_call | solution.py:356
  90.5 101.7 %backward_halo_and_reduce.1 = (f32[4,96,768]{2,1,0:T(8,128)}, bf16[1024,1536]{1,0:T(8,128)(2,1)}, bf16[1024,1536]{1,0:T(8,128)(2,1)}) custom-call(bf16[1024,768]{1,0:T(8,128)(2,1)} %get-tuple-element.11.hg_ref, bf16[1024,1536]{1,0:T(8,128)(2,1)} %get-tuple-element.12.acted_hbm, bf16[1024,1536]{1,0:T(8,128)(2,1)} %bitcast.11, ...), custom_call_target="tpu_custom_call" | custom-call | tf_op jit(solution)/shard_map/backward_halo_and_reduce/pallas_call | solution.py:609
  192.2 1.7 slice_bitcast_fusion.1
  193.9 2.1 %slice_bitcast_fusion = f32[96,3,768]{2,0,1:T(8,128)} fusion(f32[4,96,768]{2,1,0:T(8,128)} %get-tuple-element.17), kind=kLoop, calls=%fused_computation | loop fusion | bytes 1769472 | tf_op jit(solution)/shard_map/transpose | solution.py:655
  196.1 0.0 copy-start
  196.1 3.9 %copy.10 = bf16[2,512,1536]{2,1,0:T(8,128)(2,1)} copy(bf16[2,512,1536]{2,1,0:T(8,128)(2,1)} %bitcast.13) | data formatting | bytes 6291456
  200.0 0.0 copy-done
  200.0 1.7 copy.11
Async XLA Ops:
  196.1 3.9 %copy-start = (bf16[1024,1536]{1,0:T(8,128)(2,1)S(1)}, bf16[1024,1536]{1,0:T(8,128)(2,1)}, u32[]{:S(2)}) copy-start(bf16[1024,1536]{1,0:T(8,128)(2,1)} %get-tuple-element.16) | copy-start | bytes 9437188
